TPU v7x, 128 devices: a whole 4x4x4 slice. The times are simulated.
128 devices in a mesh: rows: 8 (over x, z_lo), cols: 16 (over y, z_hi, core).
Axes of the slice: x: 4, y: 4, z: 4 (z_hi: 2, z_lo: 2; z = z_hi * 2 + z_lo), core: 2. Of those that a mesh axis runs over, the one named last changes fastest.
Arguments:
- object_tiles: float32 [2, 2, 6144, 12288], P(None, None, 'rows', 'cols'), may hold values from -6 to 6
- probe: float32 [2, 512, 512], replicated, may hold values from -6 to 6
- prop_phase: float32 [512, 512], replicated, may hold values from -3.140625 to 3.140625
- amplitudes: bfloat16 [8, 16, 1, 512, 512], P('rows', 'cols'), may hold values from 0 to 2
- offsets: int32 [8, 16, 1, 2], P('rows', 'cols'), may hold values from 0 to 512
- counts: int32 [8, 16], P('rows', 'cols'), may hold values from 0 to 1
- step_size: float32 [2], replicated, may hold values from 0.3 to 1
Outputs:
- updated: float32 [2, 2, 6144, 12288], P(None, None, 'rows', 'cols')
Inputs may be any that keep to these rules, and one draw needn't show every extreme that they name: `offsets`: row and column of a window's first cell in the device's tile extended by 128 cells on every side. `counts`: slots at or past a tile's count are ignored; a tile may have no probe position.
All inputs are finite; a program needn't handle non-finite values.
Results may differ from a plain program's by a relative error of at most 0.013.
The roundings to bfloat16 on the way count: a program that leaves them out, or rounds other values in their place, can miss the bound.
Values sent between devices are 32-bit elements; how exact they have to be, the bound alone decides.
No kernel may reach another device: no remote copies, remote signals or barrier semaphores. Data moves between devices by JAX's collectives and lax.ppermute only.
A program may use at most 192 MiB of HBM per device.

v0:
```python
import math

import jax
import jax.numpy as jnp
from jax import lax
from jax.experimental import pallas as pl
from jax.experimental.pallas import tpu as pltpu
from jax.sharding import PartitionSpec as P

H = 128
W = 512
T = 768
B = 128
HALF = W // 2
LAST = T // H - 1
R0, C0, PR0, PC0, FR0, FC0, LIVE, ODD, CORE = range(9)

F32, BF16 = jnp.float32, jnp.bfloat16
WINDOW = jax.ShapeDtypeStruct((2, W, W), F32)
STRIP = jax.ShapeDtypeStruct((2, H, W), F32)
ENDS = jax.ShapeDtypeStruct((2, 2, 2 * H, H), F32)
MIDDLE = jax.ShapeDtypeStruct((2, 2, T - 2 * H, H), F32)


def rows_below(shape, first, limit):
    return lax.broadcasted_iota(jnp.int32, shape, 0) + first < limit


def cols_below(shape, first, limit):
    return lax.broadcasted_iota(jnp.int32, shape, 1) + first < limit


def params(limit_mib):
    return pltpu.CompilerParams(vmem_limit_bytes=limit_mib << 20)


def vmem():
    return pl.BlockSpec(memory_space=pltpu.VMEM)


def smem():
    return pl.BlockSpec(memory_space=pltpu.SMEM)


def sine_cosine(x, quadrant):
    y = x * x
    s = x * (1.0 + y * (-1.0 / 6 + y * (1.0 / 120 + y * (-1.0 / 5040 + y * (1.0 / 362880)))))
    c = 1.0 + y * (-0.5 + y * (1.0 / 24 + y * (-1.0 / 720 + y * (1.0 / 40320 - y * (1.0 / 3628800)))))
    swap = (quadrant & 1) == 1
    sin = jnp.where(swap, c, s)
    cos = jnp.where(swap, s, c)
    sin = jnp.where((quadrant & 2) == 2, -sin, sin)
    cos = jnp.where(((quadrant + 1) & 2) == 2, -cos, cos)
    return sin, cos


def table(rows, first_row, row_shift, col_shift):
    p = (lax.broadcasted_iota(jnp.int32, (rows, W), 0) + (first_row - row_shift)) & (W - 1)
    k = (lax.broadcasted_iota(jnp.int32, (rows, W), 1) - col_shift) & (W - 1)
    m = (p * k) & (W - 1)
    quadrant = (m + W // 8) >> 7
    x = (m - quadrant * (W // 4)).astype(F32) * (2.0 * math.pi / W)
    sin, cos = sine_cosine(x, quadrant)
    scaling = 1.0 / math.sqrt(W)
    return (cos * scaling).astype(BF16), (-sin * scaling).astype(BF16)


def phase_kernel(meta, phase, obj, cosine, sine):
    parts = (1.5703125, 4.837512969970703e-4, 7.549789948768648e-8)
    for first in range(0, W, B):
        rows = pl.ds(first, B)
        x = phase[rows, :]
        n = jnp.floor(x * (2.0 / math.pi) + 0.5)
        for part in parts:
            x = x - n * part
        sine[rows, :], cosine[rows, :] = sine_cosine(x, n.astype(jnp.int32))


def scalars_kernel(own, mate, far, count, odd, core, meta):
    meta[R0], meta[C0] = own[0], own[1]
    meta[PR0], meta[PC0] = mate[0], mate[1]
    meta[FR0], meta[FC0] = far[0], far[1]
    meta[LIVE], meta[ODD], meta[CORE] = count[0], odd[0], core[0]


def scalars(*operands):
    return pl.pallas_call(
        scalars_kernel,
        out_shape=jax.ShapeDtypeStruct((9,), jnp.int32),
        in_specs=[smem()] * 6,
        out_specs=smem(),
        compiler_params=params(1),
        name="scalars",
    )(*operands)


def forward_kernel(meta, probe, la, rb, q):
    r0, c0 = meta[R0], meta[C0]
    for first in range(0, W, B):
        rows = pl.ds(first, B)
        later = pl.ds(W + first, B)
        la[rows, :W], la[rows, W:] = table(B, first, 0, r0)
        rb[rows, :], rb[later, :] = table(B, first, c0, 0)
    for part in range(2):
        q[part] = pltpu.roll(pltpu.roll(probe[part], r0 & (W - 1), 0), c0 & (W - 1), 1)


def inverse_kernel(meta, lai, rbi):
    r0, c0 = meta[R0], meta[C0]
    for first in range(0, W, B):
        rows = pl.ds(first, B)
        later = pl.ds(W + first, B)
        lai[rows, :W], lai[rows, W:] = table(B, first, r0, 0)
        rbi[rows, :], rbi[later, :] = table(B, first, 0, c0)


PLANE = jax.ShapeDtypeStruct((W, W), F32)
LEFT = jax.ShapeDtypeStruct((W, 2 * W), BF16)
RIGHT = jax.ShapeDtypeStruct((2 * W, W), BF16)


def whole(kernel, name, out_shape, *operands, limit=16, **more):
    return pl.pallas_call(
        kernel,
        out_shape=out_shape,
        in_specs=[smem()] + [vmem()] * (len(operands) - 1),
        out_specs=[vmem()] * len(out_shape),
        compiler_params=params(limit),
        name=name,
        **more,
    )(*operands)


def edges_kernel(pieces, core, obj, near, wide, sem):
    far_side = pl.multiple_of((1 - core[0]) * (T - H), H)
    columns = [pl.ds(far_side, H), pl.ds(pl.multiple_of(T - H - far_side, H), H)]
    copies = []
    for rows, place in pieces:
        for out, cols in zip((near, wide), columns):
            source = obj.at[:, :, pl.ds(rows, place.size), cols]
            copies.append(pltpu.make_async_copy(source, out.at[:, :, place, :], sem.at[len(copies)]))
    for copy in copies:
        copy.start()
    for copy in copies:
        copy.wait()


def edges(shape, pieces, core, obj):
    return pl.pallas_call(
        lambda *refs: edges_kernel(pieces, *refs),
        out_shape=[shape] * 2,
        in_specs=[smem(), pl.BlockSpec(memory_space=pl.ANY)],
        out_specs=[vmem()] * 2,
        scratch_shapes=[pltpu.SemaphoreType.DMA((2 * len(pieces),))],
        compiler_params=params(56),
        name="edges",
    )(core, obj)


def by_side(meta, near, wide):
    first = meta[CORE] == 0
    return jnp.where(first, wide, near), jnp.where(first, near, wide)


def pack(tile, left, right, c0):
    shape = (tile.shape[0], H)
    middle = (tile.shape[0], W - 2 * H)
    a = jnp.where(cols_below(shape, 0, c0), tile[:, W - H : W], left)
    b = jnp.where(cols_below(middle, H, c0), tile[:, W:], tile[:, : W - 2 * H])
    c = jnp.where(cols_below(shape, W - H, c0), right, tile[:, W - 2 * H : W - H])
    return a, b, c


def put(out, rows, pieces):
    a, b, c = pieces
    out[rows, :H] = a
    out[rows, H : W - H] = b
    out[rows, W - H :] = c


def mate_takes(meta):
    upper = (meta[PR0] < HALF).astype(jnp.int32)
    return upper + meta[ODD] == 1


def far_takes(meta):
    upper = (meta[FR0] < HALF).astype(jnp.int32)
    return upper + meta[ODD] != 1


def pack_edge(meta, out, s, obj, near, wide, last, c0):
    rows = pl.ds(pl.multiple_of(last * (T - H), H), H)
    ends = pl.ds(pl.multiple_of(last * H, H), H)
    for part in range(2):
        sides = by_side(meta, near[s, part, ends, :], wide[s, part, ends, :])
        put(out.at[part], slice(None), pack(obj[s, part, rows, :], *sides, c0))


def far_kernel(s, meta, obj, near, wide, out):
    pack_edge(meta, out, s, obj, near, wide, meta[ODD], meta[FC0])


def mate_kernel(s, meta, obj, near, wide, passing, out):
    own = mate_takes(meta)

    @pl.when(own)
    def _():
        pack_edge(meta, out, s, obj, near, wide, 1 - meta[ODD], meta[PC0])

    @pl.when(jnp.logical_not(own))
    def _():
        out[...] = passing[...]


def beside_rows(meta, s, part, first, near, wide, near_ends, wide_ends):
    if first in (0, T - B):
        rows = pl.ds(min(first, H), B)
        return by_side(meta, near_ends[s, part, rows, :], wide_ends[s, part, rows, :])
    rows = pl.ds(first - H, B)
    return by_side(meta, near[s, part, rows, :], wide[s, part, rows, :])


def local_kernel(s, meta, obj, near_ends, wide_ends, near, wide, out):
    r0, c0 = meta[R0], meta[C0]
    for part in range(2):

        def packed(first):
            rows = pl.ds(first, B)
            sides = beside_rows(meta, s, part, first, near, wide, near_ends, wide_ends)
            return pack(obj[s, part, rows, :], *sides, c0)

        put(out.at[part], pl.ds(0, B), packed(W - H))
        for first in range(B, W - B, B):
            low, high = packed(first - H), packed(first + W - H)
            put(
                out.at[part],
                pl.ds(first, B),
                [jnp.where(rows_below(x.shape, first, r0), y, x) for x, y in zip(low, high)],
            )
        put(out.at[part], pl.ds(W - B, B), packed(W - B - H))


def far_strip(s, *args):
    return whole(lambda *refs: far_kernel(s, *refs), "far_strip", [STRIP], *args)[0]


def mate_strip(s, *args):
    return whole(lambda *refs: mate_kernel(s, *refs), "mate_strip", [STRIP], *args)[0]


def local_window(s, *args):
    return whole(lambda *refs: local_kernel(s, *refs), "local_window", [WINDOW], *args)[0]


def window_rows(meta, local, strip, part, first):
    x = local[part, pl.ds(first, B), :]
    if first == 0:
        x = jnp.where(rows_below(x.shape, first, meta[R0]), x, strip[part])
    if first == W - B:
        x = jnp.where(rows_below(x.shape, first, meta[R0]), strip[part], x)
    return x


def put_left(v4, first, re, im, inverse):
    re, im = re.astype(BF16), im.astype(BF16)
    rows, later = pl.ds(first, B), pl.ds(W + first, B)
    v4[rows, :W] = re
    v4[rows, W:] = im
    v4[later, :W] = im if inverse else -im
    v4[later, W:] = -re if inverse else re


def left_product(table, v4, m4, inverse):
    for first in range(0, W, W):
        rows, later = pl.ds(first, W), pl.ds(W + first, W)
        mid = jnp.dot(table[rows, :], v4[...], preferred_element_type=F32).astype(BF16)
        re, im = mid[:, :W], mid[:, W:]
        m4[rows, :W] = re
        m4[rows, W:] = im if inverse else -im
        m4[later, :W] = im
        m4[later, W:] = -re if inverse else re


def right_product(m4, table, first):
    re = jnp.dot(m4[pl.ds(first, B), :], table[...], preferred_element_type=F32)
    im = jnp.dot(m4[pl.ds(W + first, B), :], table[...], preferred_element_type=F32)
    return re, im


def first_kernel(meta, local, strip, q, kern_re, kern_im, la, lai, rb, rbi, psi, v4, m4):
    for first in range(0, W, B):
        rows = pl.ds(first, B)
        o_re = window_rows(meta, local, strip, 0, first)
        o_im = window_rows(meta, local, strip, 1, first)
        q_re, q_im = q[0, rows, :], q[1, rows, :]
        put_left(v4, first, q_re * o_re - q_im * o_im, q_re * o_im + q_im * o_re, False)
    left_product(la, v4, m4, False)
    for first in range(0, W, B):
        rows = pl.ds(first, B)
        re, im = right_product(m4, rb, first)
        k_re, k_im = kern_re[rows, :], kern_im[rows, :]
        put_left(v4, first, re * k_re - im * k_im, re * k_im + im * k_re, True)
    left_product(lai, v4, m4, True)
    for first in range(0, W, B):
        rows = pl.ds(first, B)
        psi[0, rows, :], psi[1, rows, :] = right_product(m4, rbi, first)


def edge_rows(meta, g, zg):
    keep_first = meta[R0] < HALF
    live = meta[LIVE] > 0

    @pl.when(keep_first)
    def _():
        for part in range(2):
            x = g[part, :H, :]
            hide = rows_below(x.shape, 0, meta[R0])
            zg[part] = jnp.where(jnp.logical_and(live, jnp.logical_not(hide)), x, 0.0)

    @pl.when(jnp.logical_not(keep_first))
    def _():
        for part in range(2):
            x = g[part, W - H :, :]
            show = rows_below(x.shape, W - H, meta[R0])
            zg[part] = jnp.where(jnp.logical_and(live, show), x, 0.0)


def second_kernel(meta, local, strip, psi, amp, la, lai, rb, rbi, g2, back, zg, v4, m4):
    for first in range(0, W, B):
        rows = pl.ds(first, B)
        o_re = window_rows(meta, local, strip, 0, first)
        o_im = window_rows(meta, local, strip, 1, first)
        p_re, p_im = psi[0, rows, :], psi[1, rows, :]
        put_left(v4, first, p_re * o_re - p_im * o_im, p_re * o_im + p_im * o_re, False)
    left_product(la, v4, m4, False)
    for first in range(0, W, B):
        rows = pl.ds(first, B)
        re, im = right_product(m4, rb, first)
        factor = 1.0 - amp[rows, :].astype(F32) / jnp.sqrt(re * re + im * im + 1.0)
        put_left(v4, first, re * factor, im * factor, True)
    left_product(lai, v4, m4, True)
    for first in range(0, W, B):
        rows = pl.ds(first, B)
        re, im = right_product(m4, rbi, first)
        p_re, p_im = psi[0, rows, :], psi[1, rows, :]
        g2[0, rows, :] = p_re * re + p_im * im
        g2[1, rows, :] = p_re * im - p_im * re
        o_re = window_rows(meta, local, strip, 0, first)
        o_im = window_rows(meta, local, strip, 1, first)
        back[0, rows, :] = (o_re * re + o_im * im).astype(BF16)
        back[1, rows, :] = (o_re * im - o_im * re).astype(BF16)
    edge_rows(meta, g2, zg)


def third_kernel(meta, back, q, kern_re, kern_im, la, lai, rb, rbi, g1, zg, v4, m4):
    for first in range(0, W, B):
        rows = pl.ds(first, B)
        put_left(v4, first, back[0, rows, :], back[1, rows, :], False)
    left_product(la, v4, m4, False)
    for first in range(0, W, B):
        rows = pl.ds(first, B)
        re, im = right_product(m4, rb, first)
        k_re, k_im = kern_re[rows, :], kern_im[rows, :]
        put_left(v4, first, re * k_re + im * k_im, im * k_re - re * k_im, True)
    left_product(lai, v4, m4, True)
    for first in range(0, W, B):
        rows = pl.ds(first, B)
        re, im = right_product(m4, rbi, first)
        q_re, q_im = q[0, rows, :], q[1, rows, :]
        g1[0, rows, :] = q_re * re + q_im * im
        g1[1, rows, :] = q_re * im - q_im * re
    edge_rows(meta, g1, zg)


def transforms(kernel, name, out_shape, meta, *operands):
    return pl.pallas_call(
        kernel,
        out_shape=out_shape,
        in_specs=[smem()] + [vmem()] * len(operands),
        out_specs=[vmem()] * len(out_shape),
        scratch_shapes=[pltpu.VMEM((2 * W, 2 * W), BF16), pltpu.VMEM((2 * W, 2 * W), BF16)],
        compiler_params=params(16),
        name=name,
    )(meta, *operands)


def shares(meta, part, mate, far):
    odd = meta[ODD] > 0
    mate = jnp.where(mate_takes(meta), mate[part], 0.0)
    far = jnp.where(far_takes(meta), far[part], 0.0)
    top = jnp.where(odd, mate, far)
    bottom = jnp.where(odd, far, mate)
    c_top = jnp.where(odd, meta[PC0], meta[FC0])
    c_bottom = jnp.where(odd, meta[FC0], meta[PC0])
    return (top, c_top), (bottom, c_bottom)


def left_part(x, c0):
    x = x[:, :H]
    return jnp.where(cols_below(x.shape, 0, c0), 0.0, x)


def right_part(x, c0):
    x = x[:, W - H :]
    return jnp.where(cols_below(x.shape, W - H, c0), x, 0.0)


def inner_parts(x, c0):
    low, high = x[:, H:], x[:, : W - H]
    low = jnp.where(cols_below(low.shape, H, c0), 0.0, low)
    high = jnp.where(cols_below(high.shape, 0, c0), high, 0.0)
    return low, high


def tile_rows(meta, g, part, first):
    live = meta[LIVE] > 0
    if first < W - H:
        x = g[part, pl.ds(first + H, B), :]
        hide = rows_below(x.shape, first + H, meta[R0])
        return jnp.where(jnp.logical_and(live, jnp.logical_not(hide)), x, 0.0)
    x = g[part, pl.ds(first - (W - H), B), :]
    show = rows_below(x.shape, first - (W - H), meta[R0])
    return jnp.where(jnp.logical_and(live, show), x, 0.0)


def middle_kernel(meta, g1, g2, near, wide):
    for s, g in enumerate((g1, g2)):
        for part in range(2):
            for first in range(B, T - B, B):
                x = tile_rows(meta, g, part, first)
                x = by_side(meta, left_part(x, meta[C0]), right_part(x, meta[C0]))
                rows = pl.ds(first - H, B)
                near[s, part, rows, :], wide[s, part, rows, :] = x


def corner_kernel(meta, g, mate, far, near, wide):
    for part in range(2):
        for first, (strip, c0) in zip((0, T - H), shares(meta, part, mate, far)):
            x = tile_rows(meta, g, part, first)
            a = left_part(x, meta[C0]) + left_part(strip, c0)
            b = right_part(x, meta[C0]) + right_part(strip, c0)
            rows = pl.ds(min(first, H), B)
            near[part, rows, :], wide[part, rows, :] = by_side(meta, a, b)


def own_rows(meta, g, part, first, mate, far):
    low, high = inner_parts(tile_rows(meta, g, part, first), meta[C0])
    if first in (0, T - B):
        top, bottom = shares(meta, part, mate, far)
        more = inner_parts(*(top if first == 0 else bottom))
        low, high = low + more[0], high + more[1]
    return low, high


def inner_kernel(s, meta, step, obj, g, mate, far, *rest):
    out, tile, sems = rest[-3:]
    size = step[s]
    copies = []
    for part in range(2):
        for first in range(0, T, B):
            rows = pl.ds(first, B)
            low, high = own_rows(meta, g, part, first, mate, far)
            tile[part, rows, : W - 2 * H] = obj[s, part, rows, H : W - H] - size * low[:, H:]
            tile[part, rows, W - 2 * H :] = obj[s, part, rows, W - H : T - H] - size * high[:, : W - 2 * H]
            target = out.at[s, part, rows, pl.ds(H, T - 2 * H)]
            copies.append(pltpu.make_async_copy(tile.at[part, rows, :], target, sems.at[part, first // B]))
            copies[-1].start()
    for copy in copies:
        copy.wait()


def border_kernel(s, meta, step, obj, g, mate, far, near, wide, near_ends, wide_ends, before, out, tile, sems):
    size = step[s]
    copies = []
    for part in range(2):
        for first in range(0, T, B):
            rows = pl.ds(first, B)
            low, high = own_rows(meta, g, part, first, mate, far)
            if first in (0, T - B):
                ends = pl.ds(min(first, H), B)
                received = by_side(meta, near_ends[part, ends, :], wide_ends[part, ends, :])
            else:
                received = beside_rows(meta, s, part, first, near, wide, None, None)
            for side, x in enumerate((low[:, :H], high[:, W - 2 * H :])):
                cols = pl.ds(side * (T - H), H)
                tile[side, part, rows, :] = obj[s, part, rows, cols] - size * (x + received[side])
        for side in range(2):
            target = out.at[s, part, :, pl.ds(side * (T - H), H)]
            copies.append(pltpu.make_async_copy(tile.at[side, part], target, sems.at[part, side]))
            copies[-1].start()
    for copy in copies:
        copy.wait()


def update(kernel, name, tile, sems, before, meta, step, obj, *operands):
    hbm = pl.BlockSpec(memory_space=pl.ANY)
    return pl.pallas_call(
        kernel,
        out_shape=jax.ShapeDtypeStruct(obj.shape, F32),
        in_specs=[smem()] * 2 + [vmem()] * (1 + len(operands)) + [hbm] * len(before),
        out_specs=hbm,
        scratch_shapes=[pltpu.VMEM(tile, F32), pltpu.SemaphoreType.DMA(sems)],
        input_output_aliases={3 + len(operands): 0} if before else {},
        compiler_params=params(16),
        name=name,
    )(meta, step, obj, *operands, *before)


def inner(s, before, *operands):
    kernel = lambda *refs: inner_kernel(s, *refs)
    return (update(kernel, "inner", (2, T, T - 2 * H), (2, T // B), before, *operands),)


def border(s, before, *operands):
    kernel = lambda *refs: border_kernel(s, *refs)
    return (update(kernel, "border", (2, 2, T, H), (2, 2), before, *operands),)


def per_device(object_tiles, probe, prop_phase, amplitudes, offsets, counts, step_size):
    n_rows, n_cols = lax.axis_size("rows"), lax.axis_size("cols")
    at_chip = [(i, i ^ 1) for i in range(n_cols) if i ^ 1 < n_cols]
    past_chip = [(i, i + 1) for i in range(1, n_cols - 1, 2)]
    past_chip = past_chip + [(j, i) for i, j in past_chip]
    mates = [(i, i ^ 1) for i in range(n_rows) if i ^ 1 < n_rows]
    fars = [(i, i + 1) for i in range(1, n_rows - 1, 2)]
    fars = fars + [(j, i) for i, j in fars]
    inward = [(i, i - 2) for i in range(2, n_rows, 2)] + [(i, i + 2) for i in range(1, n_rows - 2, 2)]
    outward = [(j, i) for i, j in inward]

    own = offsets.reshape(2)
    parity = lambda axis: lax.axis_index(axis).astype(jnp.int32).reshape(1) & 1
    odd, core = parity("rows"), parity("cols")
    after = lambda *values: lax.optimization_barrier(values)

    far, passing, strip, local = [[None, None] for _ in range(4)]

    def beside_cols(near, wide):
        wide = lax.ppermute(wide, "cols", past_chip)
        return lax.ppermute(near, "cols", at_chip), wide

    pieces = [(0, pl.ds(0, H)), (T - H, pl.ds(H, H))]
    first, obj, count, odd, *sent = after(
        own, object_tiles, counts.reshape(1), odd, *edges(ENDS, pieces, core, object_tiles)
    )
    beside = [lax.ppermute(first, "rows", mates), lax.ppermute(first, "rows", fars)]
    ends = beside_cols(*sent)
    first, *sent = after(first, *edges(MIDDLE, [(H, pl.ds(0, T - 2 * H))], core, obj))
    middle_wide = lax.ppermute(sent[1], "cols", past_chip)
    kernel = whole(phase_kernel, "phase", [PLANE, PLANE], first, prop_phase, object_tiles)
    first, *kernel = after(first, *kernel)
    meta = scalars(first, *beside, count, odd, core)
    middle_near, _ = after(sent[0], meta)
    middle = lax.ppermute(middle_near, "cols", at_chip), middle_wide

    for s in range(2):
        far[s] = far_strip(s, meta, object_tiles, *ends)
        passing[s] = lax.ppermute(far[s], "rows", inward)
    third, _ = after(meta, far[1])
    lai, rbi = whole(inverse_kernel, "inverse_tables", [LEFT, RIGHT], third)
    la, rb, q = whole(forward_kernel, "forward_tables", [LEFT, RIGHT, WINDOW], third, probe)
    passing[0], la, rb, q, lai, rbi, *middle = after(passing[0], la, rb, q, lai, rbi, *middle)
    strip[0] = lax.ppermute(mate_strip(0, meta, object_tiles, *ends, passing[0]), "rows", mates)
    local[0] = local_window(0, meta, object_tiles, *ends, *middle)
    local[1] = local_window(1, meta, object_tiles, *ends, *middle)
    strip[1] = lax.ppermute(mate_strip(1, meta, object_tiles, *ends, passing[1]), "rows", mates)
    tables = (la, lai, rb, rbi)

    (psi,) = transforms(first_kernel, "first", [WINDOW], meta, local[0], strip[0], q, *kernel, *tables)
    g2, back, z2 = transforms(
        second_kernel,
        "second",
        [WINDOW, jax.ShapeDtypeStruct((2, W, W), BF16), STRIP],
        meta,
        local[1],
        strip[1],
        psi,
        amplitudes[0, 0, 0],
        *tables,
    )
    g1, z1 = transforms(third_kernel, "third", [WINDOW, STRIP], meta, back, q, *kernel, *tables)

    mate, far, ends = [None, None], [None, None], [None, None]
    mate[1] = lax.ppermute(z2, "rows", mates)
    mate[0] = lax.ppermute(z1, "rows", mates)
    far[1] = lax.ppermute(mate[1], "rows", outward)
    _, *sent = after(mate[1], *whole(middle_kernel, "middle", [MIDDLE] * 2, meta, g1, g2))
    middle = beside_cols(*sent)
    far[0] = lax.ppermute(mate[0], "rows", outward)
    grads = (g1, g2)
    out = ()
    for s in (1, 0):
        shape = jax.ShapeDtypeStruct(ENDS.shape[1:], F32)
        sent = whole(corner_kernel, "corner", [shape] * 2, meta, grads[s], mate[s], far[s])
        ends[s] = beside_cols(*sent)
    for s in (1, 0):
        out = inner(s, out, meta, step_size, object_tiles, grads[s], mate[s], far[s])
    for s in (1, 0):
        out = border(s, out, meta, step_size, object_tiles, grads[s], mate[s], far[s], *middle, *ends[s])
    return out[0]


def solution(mesh):
    return jax.shard_map(
        per_device,
        mesh=mesh,
        in_specs=(
            P(None, None, "rows", "cols"),
            P(),
            P(),
            P("rows", "cols", None, None, None),
            P("rows", "cols", None, None),
            P("rows", "cols"),
            P(),
        ),
        out_specs=P(None, None, "rows", "cols"),
        check_vma=False,
    )
```

profile of v0, /device:TPU:19, one launch (start us, length us, event | category | flops | bytes accessed | tf_op | source)
XLA Modules:
  0.0 136.8 jit_solution(8830952407755884848)
XLA Ops:
  0.0 2.2 %edges.2 = (f32[2,2,256,128]{3,2,1,0:T(8,128)}, f32[2,2,256,128]{3,2,1,0:T(8,128)}) custom-call(s32[1]{0:T(128)} %bitcast.3.refs_0_.core, f32[2,2,768,768]{3,2,1,0:T(8,128)} %refs_2_.7), custom_call_target="tpu_custom_call" | custom-call | tf_op jit(solution)/shard_map/edges/pallas_call | solution.py:149
  2.3 1.7 %collective-permute-start = (s32[2]{0:T(128)S(1)}, s32[2]{0:T(128)S(1)}, u32[]{:S(2)}, u32[]{:S(2)}) collective-permute-start(s32[2]{0:T(128)S(1)} %bitcast.9), channel_id=1, source_target_pairs={{0,16},{16,0},{32,48},{48,32},{64,80},{80,64},{96,112},{112,96},{1... | collective-permute-start | bytes 32 | tf_op jit(solution)/shard_map/ppermute | solution.py:545
  4.0 2.0 %collective-permute-start.1 = (s32[2]{0:T(128)S(1)}, s32[2]{0:T(128)S(1)}, u32[]{:S(2)}, u32[]{:S(2)}) collective-permute-start(s32[2]{0:T(128)S(1)} %bitcast.10), channel_id=1, source_target_pairs={{16,32},{48,64},{80,96},{32,16},{64,48},{96,80},{17,33},{49,65},{8... | collective-permute-start | bytes 32 | tf_op jit(solution)/shard_map/ppermute | solution.py:545
  7.1 5.3 %collective-permute-start.3 = (f32[2,2,256,128]{3,2,1,0:T(8,128)}, f32[2,2,256,128]{3,2,1,0:T(8,128)S(1)}, u32[]{:S(2)}, u32[]{:S(2)}) collective-permute-start(f32[2,2,256,128]{3,2,1,0:T(8,128)} %get-tuple-element.64), channel_id=1, source_target_pairs={{1,2},{3,4},{5,6},{7,8},{9,10},{11,12},{13,14},{2,1},{4,3},{6,5},{... | collective-permute-start | bytes 1572872 | tf_op jit(solution)/shard_map/ppermute | solution.py:538
  12.4 3.0 %edges.3 = (f32[2,2,512,128]{3,2,1,0:T(8,128)}, f32[2,2,512,128]{3,2,1,0:T(8,128)}) custom-call(s32[1]{0:T(128)} %bitcast.3.refs_0_.core, f32[2,2,768,768]{3,2,1,0:T(8,128)} %refs_2_.7), custom_call_target="tpu_custom_call" | custom-call | tf_op jit(solution)/shard_map/edges/pallas_call | solution.py:149
  15.4 1.9 %collective-permute-start.6 = (f32[2,2,512,128]{3,2,1,0:T(8,128)}, f32[2,2,512,128]{3,2,1,0:T(8,128)S(1)}, u32[]{:S(2)}, u32[]{:S(2)}) collective-permute-start(f32[2,2,512,128]{3,2,1,0:T(8,128)} %get-tuple-element.73), channel_id=1, source_target_pairs={{1,2},{3,4},{5,6},{7,8},{9,10},{11,12},{13,14},{2,1},{4,3},{6,5},{... | collective-permute-start | bytes 3145736 | tf_op jit(solution)/shard_map/ppermute | solution.py:548
  18.0 3.7 %copy-done = f32[2,2,768,768]{3,2,1,0:T(8,128)S(1)} copy-done((f32[2,2,768,768]{3,2,1,0:T(8,128)S(1)}, f32[2,2,768,768]{3,2,1,0:T(8,128)}, u32[]{:S(2)}) %copy-start) | copy-done | bytes 9437208
  21.6 2.1 %phase.2 = (f32[512,512]{1,0:T(8,128)S(1)}, f32[512,512]{1,0:T(8,128)S(1)}) custom-call(s32[2]{0:T(128)S(1)} %bitcast.11, f32[512,512]{1,0:T(8,128)S(1)} %copy-done.2, f32[2,2,768,768]{3,2,1,0:T(8,128)S(1)} %copy-done), custom_call_target="tpu_custom_call" | custom-call | tf_op jit(solution)/shard_map/phase/pallas_call | solution.py:123
  25.9 10.5 %collective-permute-done.3.refs_3_ = f32[2,2,256,128]{3,2,1,0:T(8,128)S(1)} collective-permute-done((f32[2,2,256,128]{3,2,1,0:T(8,128)}, f32[2,2,256,128]{3,2,1,0:T(8,128)S(1)}, u32[]{:S(2)}, u32[]{:S(2)}) %collective-permute-start.3) | collective-permute-done | bytes 524320 | tf_op jit(solution)/shard_map/ppermute | solution.py:538
  37.0 2.3 %collective-permute-start.4 = (f32[2,128,512]{2,1,0:T(8,128)S(1)}, f32[2,128,512]{2,1,0:T(8,128)S(1)}, u32[]{:S(2)}, u32[]{:S(2)}) collective-permute-start(f32[2,128,512]{2,1,0:T(8,128)S(1)} %far_strip.2), channel_id=1, source_target_pairs={{32,0},{64,32},{96,64},{16,48},{48,80},{80,112},{33,1},{65,33},{97... | collective-permute-start | bytes 1572872 | tf_op jit(solution)/shard_map/ppermute | solution.py:557
  39.9 2.1 %collective-permute-start.7 = (f32[2,128,512]{2,1,0:T(8,128)S(1)}, f32[2,128,512]{2,1,0:T(8,128)S(1)}, u32[]{:S(2)}, u32[]{:S(2)}) collective-permute-start(f32[2,128,512]{2,1,0:T(8,128)S(1)} %far_strip.3), channel_id=1, source_target_pairs={{32,0},{64,32},{96,64},{16,48},{48,80},{80,112},{33,1},{65,33},{97... | collective-permute-start | bytes 1572872 | tf_op jit(solution)/shard_map/ppermute | solution.py:557
  42.0 3.9 %inverse_tables.1 = (bf16[512,1024]{1,0:T(8,128)(2,1)S(1)}, bf16[1024,512]{1,0:T(8,128)(2,1)S(1)}) custom-call(s32[9]{0:T(128)S(1)} %scalars.1.refs_0_.meta), custom_call_target="tpu_custom_call" | custom-call | tf_op jit(solution)/shard_map/inverse_tables/pallas_call | solution.py:123
  46.0 6.5 %forward_tables.1 = (bf16[512,1024]{1,0:T(8,128)(2,1)S(1)}, bf16[1024,512]{1,0:T(8,128)(2,1)S(1)}, f32[2,512,512]{2,1,0:T(8,128)S(1)}) custom-call(s32[9]{0:T(128)S(1)} %scalars.1.refs_0_.meta, f32[2,512,512]{2,1,0:T(8,128)S(1)} %copy-done.1), custom_call_target="tpu_custom_call" | custom-call | tf_op jit(solution)/shard_map/forward_tables/pallas_call | solution.py:123
  53.2 3.3 %collective-permute-start.9 = (f32[2,128,512]{2,1,0:T(8,128)S(1)}, f32[2,128,512]{2,1,0:T(8,128)S(1)}, u32[]{:S(2)}, u32[]{:S(2)}) collective-permute-start(f32[2,128,512]{2,1,0:T(8,128)S(1)} %mate_strip.3), channel_id=1, source_target_pairs={{0,16},{16,0},{32,48},{48,32},{64,80},{80,64},{96,112},{112,96},{1... | collective-permute-start | bytes 1572872 | tf_op jit(solution)/shard_map/ppermute | solution.py:562
  59.7 6.1 %collective-permute-done.9.strip = f32[2,128,512]{2,1,0:T(8,128)S(1)} collective-permute-done((f32[2,128,512]{2,1,0:T(8,128)S(1)}, f32[2,128,512]{2,1,0:T(8,128)S(1)}, u32[]{:S(2)}, u32[]{:S(2)}) %collective-permute-start.9) | collective-permute-done | bytes 524320 | tf_op jit(solution)/shard_map/ppermute | solution.py:562
  65.8 5.6 %first.1.psi = f32[2,512,512]{2,1,0:T(8,128)S(1)} custom-call(s32[9]{0:T(128)S(1)} %scalars.1.refs_0_.meta, f32[2,512,512]{2,1,0:T(8,128)S(1)} %local_window.3.local, f32[2,128,512]{2,1,0:T(8,128)S(1)} %collective-permute-done.9.strip, f32[2,512,512]{2,1,0:T(8,128)S(1)} %get-tuple-element.77.q, f32[512,512]{1,0:T(8,128)S(1)} %get-tuple-element.78.kern_re, ...), custom_call_target="tpu_custom_call" | custom-call | tf_op jit(solution)/shard_map/first/pallas_call | solution.py:376
  71.5 6.8 %second.1 = (f32[2,512,512]{2,1,0:T(8,128)S(1)}, bf16[2,512,512]{2,1,0:T(8,128)(2,1)S(1)}, f32[2,128,512]{2,1,0:T(8,128)S(1)}) custom-call(s32[9]{0:T(128)S(1)} %scalars.1.refs_0_.meta, f32[2,512,512]{2,1,0:T(8,128)S(1)} %local_window.2.local, f32[2,128,512]{2,1,0:T(8,128)S(1)} %collective-permute-done.8.strip, f32[2,512,512]{2,1,0:T(8,128)S(1)} %first.1.psi, ...), custom_call_target="tpu_custom_call" | custom-call | tf_op jit(solution)/shard_map/second/pallas_call | solution.py:376
  79.0 5.8 %third.1 = (f32[2,512,512]{2,1,0:T(8,128)S(1)}, f32[2,128,512]{2,1,0:T(8,128)S(1)}) custom-call(s32[9]{0:T(128)S(1)} %scalars.1.refs_0_.meta, bf16[2,512,512]{2,1,0:T(8,128)(2,1)S(1)} %get-tuple-element.84.back, f32[2,512,512]{2,1,0:T(8,128)S(1)} %get-tuple-element.77.q, f32[512,512]{1,0:T(8,128)S(1)} %get-tuple-element.78.kern_re, ...), custom_call_target="tpu_custom_call" | custom-call | tf_op jit(solution)/shard_map/third/pallas_call | solution.py:376
  86.8 4.0 %collective-permute-done.12.mate.refs_4_ = f32[2,128,512]{2,1,0:T(8,128)S(1)} collective-permute-done((f32[2,128,512]{2,1,0:T(8,128)S(1)}, f32[2,128,512]{2,1,0:T(8,128)S(1)}, u32[]{:S(2)}, u32[]{:S(2)}) %collective-permute-start.12) | collective-permute-done | bytes 524320 | tf_op jit(solution)/shard_map/ppermute | solution.py:583
  90.8 3.7 %collective-permute-start.17 = (f32[2,128,512]{2,1,0:T(8,128)S(1)}, f32[2,128,512]{2,1,0:T(8,128)S(1)}, u32[]{:S(2)}, u32[]{:S(2)}) collective-permute-start(f32[2,128,512]{2,1,0:T(8,128)S(1)} %collective-permute-done.12.mate.refs_4_), channel_id=1, source_target_pairs={{0,32},{32,64},{64,96},{48,16},{80,48},{112,80},{1,33},{33,65},{65... | collective-permute-start | bytes 1572872 | tf_op jit(solution)/shard_map/ppermute | solution.py:585
  94.4 1.9 %collective-permute-start.14 = (f32[2,2,512,128]{3,2,1,0:T(8,128)S(1)}, f32[2,2,512,128]{3,2,1,0:T(8,128)S(1)}, u32[]{:S(2)}, u32[]{:S(2)}) collective-permute-start(f32[2,2,512,128]{3,2,1,0:T(8,128)S(1)} %get-tuple-element.92), channel_id=1, source_target_pairs={{1,2},{3,4},{5,6},{7,8},{9,10},{11,12},{13,14},{2,1},{4,3},{6,5},{... | collective-permute-start | bytes 3145736 | tf_op jit(solution)/shard_map/ppermute | solution.py:538
  96.7 3.7 %collective-permute-start.11 = (f32[2,128,512]{2,1,0:T(8,128)S(1)}, f32[2,128,512]{2,1,0:T(8,128)S(1)}, u32[]{:S(2)}, u32[]{:S(2)}) collective-permute-start(f32[2,128,512]{2,1,0:T(8,128)S(1)} %collective-permute-done.10.mate.refs_4_), channel_id=1, source_target_pairs={{0,32},{32,64},{64,96},{48,16},{80,48},{112,80},{1,33},{33,65},{65... | collective-permute-start | bytes 1572872 | tf_op jit(solution)/shard_map/ppermute | solution.py:588
  100.4 5.3 %collective-permute-done.17.far.refs_5_ = f32[2,128,512]{2,1,0:T(8,128)S(1)} collective-permute-done((f32[2,128,512]{2,1,0:T(8,128)S(1)}, f32[2,128,512]{2,1,0:T(8,128)S(1)}, u32[]{:S(2)}, u32[]{:S(2)}) %collective-permute-start.17) | collective-permute-done | bytes 524320 | tf_op jit(solution)/shard_map/ppermute | solution.py:585
  106.4 2.4 %collective-permute-start.18 = (f32[2,256,128]{2,1,0:T(8,128)S(1)}, f32[2,256,128]{2,1,0:T(8,128)S(1)}, u32[]{:S(2)}, u32[]{:S(2)}) collective-permute-start(f32[2,256,128]{2,1,0:T(8,128)S(1)} %get-tuple-element.95), channel_id=1, source_target_pairs={{0,1},{1,0},{2,3},{3,2},{4,5},{5,4},{6,7},{7,6},{8,9},{9,8},{10,11... | collective-permute-start | bytes 786440 | tf_op jit(solution)/shard_map/ppermute | solution.py:539
  108.7 1.9 %collective-permute-start.19 = (f32[2,256,128]{2,1,0:T(8,128)S(1)}, f32[2,256,128]{2,1,0:T(8,128)S(1)}, u32[]{:S(2)}, u32[]{:S(2)}) collective-permute-start(f32[2,256,128]{2,1,0:T(8,128)S(1)} %get-tuple-element.96), channel_id=1, source_target_pairs={{1,2},{3,4},{5,6},{7,8},{9,10},{11,12},{13,14},{2,1},{4,3},{6,5},{... | collective-permute-start | bytes 786440 | tf_op jit(solution)/shard_map/ppermute | solution.py:538
  110.7 6.2 %collective-permute-done.11.far.refs_5_ = f32[2,128,512]{2,1,0:T(8,128)S(1)} collective-permute-done((f32[2,128,512]{2,1,0:T(8,128)S(1)}, f32[2,128,512]{2,1,0:T(8,128)S(1)}, u32[]{:S(2)}, u32[]{:S(2)}) %collective-permute-start.11) | collective-permute-done | bytes 524320 | tf_op jit(solution)/shard_map/ppermute | solution.py:588
  119.0 2.0 %collective-permute-start.16 = (f32[2,256,128]{2,1,0:T(8,128)S(1)}, f32[2,256,128]{2,1,0:T(8,128)S(1)}, u32[]{:S(2)}, u32[]{:S(2)}) collective-permute-start(f32[2,256,128]{2,1,0:T(8,128)S(1)} %get-tuple-element.94), channel_id=1, source_target_pairs={{1,2},{3,4},{5,6},{7,8},{9,10},{11,12},{13,14},{2,1},{4,3},{6,5},{... | collective-permute-start | bytes 786440 | tf_op jit(solution)/shard_map/ppermute | solution.py:538
  121.0 2.5 %inner.2.refs_6_ = f32[2,2,768,768]{3,2,1,0:T(8,128)} custom-call(s32[9]{0:T(128)S(1)} %scalars.1.refs_0_.meta, f32[2]{0:T(128)S(1)} %copy-done.4, f32[2,2,768,768]{3,2,1,0:T(8,128)S(1)} %bitcast.7, f32[2,512,512]{2,1,0:T(8,128)S(1)} %get-tuple-element.88.g2.g.refs_3_, f32[2,128,512]{2,1,0:T(8,128)S(1)} %collective-permute-done.12.mate.refs_4_, ...), custom_call_target="tpu_custom_call" | custom-call | tf_op jit(solution)/shard_map/inner/pallas_call | solution.py:497
  123.5 2.5 %inner.3.refs_10_ = f32[2,2,768,768]{3,2,1,0:T(8,128)} custom-call(s32[9]{0:T(128)S(1)} %scalars.1.refs_0_.meta, f32[2]{0:T(128)S(1)} %copy-done.4, f32[2,2,768,768]{3,2,1,0:T(8,128)S(1)} %bitcast.7, f32[2,512,512]{2,1,0:T(8,128)S(1)} %get-tuple-element.85.g1.g.refs_3_, ...), custom_call_target="tpu_custom_call", output_to_operand_aliasing={{}: (6, {})} | custom-call | tf_op jit(solution)/shard_map/inner/pallas_call | solution.py:497
  126.0 5.8 %collective-permute-done.19.refs_9_ = f32[2,256,128]{2,1,0:T(8,128)S(1)} collective-permute-done((f32[2,256,128]{2,1,0:T(8,128)S(1)}, f32[2,256,128]{2,1,0:T(8,128)S(1)}, u32[]{:S(2)}, u32[]{:S(2)}) %collective-permute-start.19) | collective-permute-done | bytes 262176 | tf_op jit(solution)/shard_map/ppermute | solution.py:538
  131.7 2.0 %border.2.refs_10_ = f32[2,2,768,768]{3,2,1,0:T(8,128)} custom-call(s32[9]{0:T(128)S(1)} %scalars.1.refs_0_.meta, f32[2]{0:T(128)S(1)} %copy-done.4, f32[2,2,768,768]{3,2,1,0:T(8,128)S(1)} %bitcast.7, f32[2,512,512]{2,1,0:T(8,128)S(1)} %get-tuple-element.88.g2.g.refs_3_, ...), custom_call_target="tpu_custom_call", output_to_operand_aliasing={{}: (10, {})} | custom-call | tf_op jit(solution)/shard_map/border/pallas_call | solution.py:497
  134.5 2.0 %border.3 = f32[2,2,768,768]{3,2,1,0:T(8,128)} custom-call(s32[9]{0:T(128)S(1)} %scalars.1.refs_0_.meta, f32[2]{0:T(128)S(1)} %copy-done.4, f32[2,2,768,768]{3,2,1,0:T(8,128)S(1)} %bitcast.7, f32[2,512,512]{2,1,0:T(8,128)S(1)} %get-tuple-element.85.g1.g.refs_3_, ...), custom_call_target="tpu_custom_call", output_to_operand_aliasing={{}: (10, {})} | custom-call | tf_op jit(solution)/shard_map/border/pallas_call | solution.py:497
  (51 shorter events, 14.9 us)
Async XLA Ops:
  0.0 2.2 %copy-start.5 = (s32[1,1,1,2]{3,2,1,0:T(1,128)S(1)}, s32[1,1,1,2]{3,2,1,0:T(1,128)}, u32[]{:S(2)}) copy-start(s32[1,1,1,2]{3,2,1,0:T(1,128)} %param.11) | copy-start | bytes 28
  2.3 15.7 %copy-start.2 = (f32[512,512]{1,0:T(8,128)S(1)}, f32[512,512]{1,0:T(8,128)}, u32[]{:S(2)}) copy-start(f32[512,512]{1,0:T(8,128)} %phase.3) | copy-start | bytes 3145732
  2.3 21.5 %collective-permute-start = (s32[2]{0:T(128)S(1)}, s32[2]{0:T(128)S(1)}, u32[]{:S(2)}, u32[]{:S(2)}) collective-permute-start(s32[2]{0:T(128)S(1)} %bitcast.9), channel_id=1, source_target_pairs={{0,16},{16,0},{32,48},{48,32},{64,80},{80,64},{96,112},{112,96},{1... | collective-permute-start | bytes 32 | tf_op jit(solution)/shard_map/ppermute | solution.py:545
  4.0 19.8 %collective-permute-start.1 = (s32[2]{0:T(128)S(1)}, s32[2]{0:T(128)S(1)}, u32[]{:S(2)}, u32[]{:S(2)}) collective-permute-start(s32[2]{0:T(128)S(1)} %bitcast.10), channel_id=1, source_target_pairs={{16,32},{48,64},{80,96},{32,16},{64,48},{96,80},{17,33},{49,65},{8... | collective-permute-start | bytes 32 | tf_op jit(solution)/shard_map/ppermute | solution.py:545
  6.0 19.8 %collective-permute-start.2 = (f32[2,2,256,128]{3,2,1,0:T(8,128)}, f32[2,2,256,128]{3,2,1,0:T(8,128)S(1)}, u32[]{:S(2)}, u32[]{:S(2)}) collective-permute-start(f32[2,2,256,128]{3,2,1,0:T(8,128)} %get-tuple-element.63), channel_id=1, source_target_pairs={{0,1},{1,0},{2,3},{3,2},{4,5},{5,4},{6,7},{7,6},{8,9},{9,8},{10,11... | collective-permute-start | bytes 1572872 | tf_op jit(solution)/shard_map/ppermute | solution.py:539
  7.1 29.2 %collective-permute-start.3 = (f32[2,2,256,128]{3,2,1,0:T(8,128)}, f32[2,2,256,128]{3,2,1,0:T(8,128)S(1)}, u32[]{:S(2)}, u32[]{:S(2)}) collective-permute-start(f32[2,2,256,128]{3,2,1,0:T(8,128)} %get-tuple-element.64), channel_id=1, source_target_pairs={{1,2},{3,4},{5,6},{7,8},{9,10},{11,12},{13,14},{2,1},{4,3},{6,5},{... | collective-permute-start | bytes 1572872 | tf_op jit(solution)/shard_map/ppermute | solution.py:538
  15.4 37.1 %collective-permute-start.6 = (f32[2,2,512,128]{3,2,1,0:T(8,128)}, f32[2,2,512,128]{3,2,1,0:T(8,128)S(1)}, u32[]{:S(2)}, u32[]{:S(2)}) collective-permute-start(f32[2,2,512,128]{3,2,1,0:T(8,128)} %get-tuple-element.73), channel_id=1, source_target_pairs={{1,2},{3,4},{5,6},{7,8},{9,10},{11,12},{13,14},{2,1},{4,3},{6,5},{... | collective-permute-start | bytes 3145736 | tf_op jit(solution)/shard_map/ppermute | solution.py:548
  18.0 3.7 %copy-start = (f32[2,2,768,768]{3,2,1,0:T(8,128)S(1)}, f32[2,2,768,768]{3,2,1,0:T(8,128)}, u32[]{:S(2)}) copy-start(f32[2,2,768,768]{3,2,1,0:T(8,128)} %refs_2_.7) | copy-start | bytes 28311556
  21.6 3.3 %copy-start.6 = (f32[2,2,512,128]{3,2,1,0:T(8,128)S(1)}, f32[2,2,512,128]{3,2,1,0:T(8,128)}, u32[]{:S(2)}) copy-start(f32[2,2,512,128]{3,2,1,0:T(8,128)} %get-tuple-element.72) | copy-start | bytes 3145732
  25.0 27.5 %collective-permute-start.5 = (f32[2,2,512,128]{3,2,1,0:T(8,128)S(1)}, f32[2,2,512,128]{3,2,1,0:T(8,128)S(1)}, u32[]{:S(2)}, u32[]{:S(2)}) collective-permute-start(f32[2,2,512,128]{3,2,1,0:T(8,128)S(1)} %copy-done.6), channel_id=1, source_target_pairs={{0,1},{1,0},{2,3},{3,2},{4,5},{5,4},{6,7},{7,6},{8,9},{9,8},{10,11... | collective-permute-start | bytes 3145736 | tf_op jit(solution)/shard_map/ppermute | solution.py:553
  36.3 16.2 %slice-start = ((s8[9437184]{0:T(1024)(128)(4,1)}), s8[4194304]{0:T(1024)(128)(4,1)S(1)}, s32[]{:S(2)}) async-start(s8[9437184]{0:T(1024)(128)(4,1)} %bitcast.6), calls=%async_computation | async-start | bytes 8388608
  36.3 16.2 %slice-start.1 = ((s8[9437184]{0:T(1024)(128)(4,1)}), s8[4194304]{0:T(1024)(128)(4,1)S(1)}, s32[]{:S(2)}) async-start(s8[9437184]{0:T(1024)(128)(4,1)} %bitcast.6), calls=%async_computation.1 | async-start | bytes 8388608
  36.9 9.0 %copy-start.1 = (f32[2,512,512]{2,1,0:T(8,128)S(1)}, f32[2,512,512]{2,1,0:T(8,128)}, u32[]{:S(2)}) copy-start(f32[2,512,512]{2,1,0:T(8,128)} %probe.1) | copy-start | bytes 6291460
  37.0 15.6 %slice-start.2 = ((s8[9437184]{0:T(1024)(128)(4,1)}), s8[1048576]{0:T(1024)(128)(4,1)S(1)}, s32[]{:S(2)}) async-start(s8[9437184]{0:T(1024)(128)(4,1)} %bitcast.6), calls=%async_computation.2 | async-start | bytes 2097152
  37.0 15.5 %collective-permute-start.4 = (f32[2,128,512]{2,1,0:T(8,128)S(1)}, f32[2,128,512]{2,1,0:T(8,128)S(1)}, u32[]{:S(2)}, u32[]{:S(2)}) collective-permute-start(f32[2,128,512]{2,1,0:T(8,128)S(1)} %far_strip.2), channel_id=1, source_target_pairs={{32,0},{64,32},{96,64},{16,48},{48,80},{80,112},{33,1},{65,33},{97... | collective-permute-start | bytes 1572872 | tf_op jit(solution)/shard_map/ppermute | solution.py:557
  39.9 16.5 %collective-permute-start.7 = (f32[2,128,512]{2,1,0:T(8,128)S(1)}, f32[2,128,512]{2,1,0:T(8,128)S(1)}, u32[]{:S(2)}, u32[]{:S(2)}) collective-permute-start(f32[2,128,512]{2,1,0:T(8,128)S(1)} %far_strip.3), channel_id=1, source_target_pairs={{32,0},{64,32},{96,64},{16,48},{48,80},{80,112},{33,1},{65,33},{97... | collective-permute-start | bytes 1572872 | tf_op jit(solution)/shard_map/ppermute | solution.py:557
  53.2 12.6 %collective-permute-start.9 = (f32[2,128,512]{2,1,0:T(8,128)S(1)}, f32[2,128,512]{2,1,0:T(8,128)S(1)}, u32[]{:S(2)}, u32[]{:S(2)}) collective-permute-start(f32[2,128,512]{2,1,0:T(8,128)S(1)} %mate_strip.3), channel_id=1, source_target_pairs={{0,16},{16,0},{32,48},{48,32},{64,80},{80,64},{96,112},{112,96},{1... | collective-permute-start | bytes 1572872 | tf_op jit(solution)/shard_map/ppermute | solution.py:562
  57.1 14.4 %collective-permute-start.8 = (f32[2,128,512]{2,1,0:T(8,128)S(1)}, f32[2,128,512]{2,1,0:T(8,128)S(1)}, u32[]{:S(2)}, u32[]{:S(2)}) collective-permute-start(f32[2,128,512]{2,1,0:T(8,128)S(1)} %mate_strip.2), channel_id=1, source_target_pairs={{0,16},{16,0},{32,48},{48,32},{64,80},{80,64},{96,112},{112,96},{1... | collective-permute-start | bytes 1572872 | tf_op jit(solution)/shard_map/ppermute | solution.py:565
  59.7 11.8 %copy-start.3 = (bf16[1,1,1,512,512]{4,3,2,1,0:T(8,128)(2,1)S(1)}, bf16[1,1,1,512,512]{4,3,2,1,0:T(8,128)(2,1)}, u32[]{:S(2)}) copy-start(bf16[1,1,1,512,512]{4,3,2,1,0:T(8,128)(2,1)} %param.10) | copy-start | bytes 1572868
  78.3 12.5 %collective-permute-start.12 = (f32[2,128,512]{2,1,0:T(8,128)S(1)}, f32[2,128,512]{2,1,0:T(8,128)S(1)}, u32[]{:S(2)}, u32[]{:S(2)}) collective-permute-start(f32[2,128,512]{2,1,0:T(8,128)S(1)} %get-tuple-element.87), channel_id=1, source_target_pairs={{0,16},{16,0},{32,48},{48,32},{64,80},{80,64},{96,112},{112,96},{1... | collective-permute-start | bytes 1572872 | tf_op jit(solution)/shard_map/ppermute | solution.py:583
  84.8 11.9 %collective-permute-start.10 = (f32[2,128,512]{2,1,0:T(8,128)S(1)}, f32[2,128,512]{2,1,0:T(8,128)S(1)}, u32[]{:S(2)}, u32[]{:S(2)}) collective-permute-start(f32[2,128,512]{2,1,0:T(8,128)S(1)} %get-tuple-element.86), channel_id=1, source_target_pairs={{0,16},{16,0},{32,48},{48,32},{64,80},{80,64},{96,112},{112,96},{1... | collective-permute-start | bytes 1572872 | tf_op jit(solution)/shard_map/ppermute | solution.py:584
  90.8 41.0 %collective-permute-start.13 = (f32[2,2,512,128]{3,2,1,0:T(8,128)S(1)}, f32[2,2,512,128]{3,2,1,0:T(8,128)S(1)}, u32[]{:S(2)}, u32[]{:S(2)}) collective-permute-start(f32[2,2,512,128]{3,2,1,0:T(8,128)S(1)} %get-tuple-element.91), channel_id=1, source_target_pairs={{0,1},{1,0},{2,3},{3,2},{4,5},{5,4},{6,7},{7,6},{8,9},{9,8},{10,11... | collective-permute-start | bytes 3145736 | tf_op jit(solution)/shard_map/ppermute | solution.py:539
  90.8 14.9 %collective-permute-start.17 = (f32[2,128,512]{2,1,0:T(8,128)S(1)}, f32[2,128,512]{2,1,0:T(8,128)S(1)}, u32[]{:S(2)}, u32[]{:S(2)}) collective-permute-start(f32[2,128,512]{2,1,0:T(8,128)S(1)} %collective-permute-done.12.mate.refs_4_), channel_id=1, source_target_pairs={{0,32},{32,64},{64,96},{48,16},{80,48},{112,80},{1,33},{33,65},{65... | collective-permute-start | bytes 1572872 | tf_op jit(solution)/shard_map/ppermute | solution.py:585
  94.4 37.3 %collective-permute-start.14 = (f32[2,2,512,128]{3,2,1,0:T(8,128)S(1)}, f32[2,2,512,128]{3,2,1,0:T(8,128)S(1)}, u32[]{:S(2)}, u32[]{:S(2)}) collective-permute-start(f32[2,2,512,128]{3,2,1,0:T(8,128)S(1)} %get-tuple-element.92), channel_id=1, source_target_pairs={{1,2},{3,4},{5,6},{7,8},{9,10},{11,12},{13,14},{2,1},{4,3},{6,5},{... | collective-permute-start | bytes 3145736 | tf_op jit(solution)/shard_map/ppermute | solution.py:538
  96.7 20.2 %collective-permute-start.11 = (f32[2,128,512]{2,1,0:T(8,128)S(1)}, f32[2,128,512]{2,1,0:T(8,128)S(1)}, u32[]{:S(2)}, u32[]{:S(2)}) collective-permute-start(f32[2,128,512]{2,1,0:T(8,128)S(1)} %collective-permute-done.10.mate.refs_4_), channel_id=1, source_target_pairs={{0,32},{32,64},{64,96},{48,16},{80,48},{112,80},{1,33},{33,65},{65... | collective-permute-start | bytes 1572872 | tf_op jit(solution)/shard_map/ppermute | solution.py:588
  106.3 14.6 %copy-start.4 = (f32[2]{0:T(128)S(1)}, f32[2]{0:T(128)}, u32[]{:S(2)}) copy-start(f32[2]{0:T(128)} %refs_1_.22) | copy-start | bytes 28
  106.4 12.7 %collective-permute-start.18 = (f32[2,256,128]{2,1,0:T(8,128)S(1)}, f32[2,256,128]{2,1,0:T(8,128)S(1)}, u32[]{:S(2)}, u32[]{:S(2)}) collective-permute-start(f32[2,256,128]{2,1,0:T(8,128)S(1)} %get-tuple-element.95), channel_id=1, source_target_pairs={{0,1},{1,0},{2,3},{3,2},{4,5},{5,4},{6,7},{7,6},{8,9},{9,8},{10,11... | collective-permute-start | bytes 786440 | tf_op jit(solution)/shard_map/ppermute | solution.py:539
  108.7 23.0 %collective-permute-start.19 = (f32[2,256,128]{2,1,0:T(8,128)S(1)}, f32[2,256,128]{2,1,0:T(8,128)S(1)}, u32[]{:S(2)}, u32[]{:S(2)}) collective-permute-start(f32[2,256,128]{2,1,0:T(8,128)S(1)} %get-tuple-element.96), channel_id=1, source_target_pairs={{1,2},{3,4},{5,6},{7,8},{9,10},{11,12},{13,14},{2,1},{4,3},{6,5},{... | collective-permute-start | bytes 786440 | tf_op jit(solution)/shard_map/ppermute | solution.py:538
  117.6 16.2 %collective-permute-start.15 = (f32[2,256,128]{2,1,0:T(8,128)S(1)}, f32[2,256,128]{2,1,0:T(8,128)S(1)}, u32[]{:S(2)}, u32[]{:S(2)}) collective-permute-start(f32[2,256,128]{2,1,0:T(8,128)S(1)} %get-tuple-element.93), channel_id=1, source_target_pairs={{0,1},{1,0},{2,3},{3,2},{4,5},{5,4},{6,7},{7,6},{8,9},{9,8},{10,11... | collective-permute-start | bytes 786440 | tf_op jit(solution)/shard_map/ppermute | solution.py:539
  119.0 15.5 %collective-permute-start.16 = (f32[2,256,128]{2,1,0:T(8,128)S(1)}, f32[2,256,128]{2,1,0:T(8,128)S(1)}, u32[]{:S(2)}, u32[]{:S(2)}) collective-permute-start(f32[2,256,128]{2,1,0:T(8,128)S(1)} %get-tuple-element.94), channel_id=1, source_target_pairs={{1,2},{3,4},{5,6},{7,8},{9,10},{11,12},{13,14},{2,1},{4,3},{6,5},{... | collective-permute-start | bytes 786440 | tf_op jit(solution)/shard_map/ppermute | solution.py:538
where the time goes:
time: 137 us
  Pallas kernels  52.8 us (39%)
  starting transfers between devices  40.1 us (29%)
  waiting for transfers between devices  38.9 us (28%)
  local copies, waits for them, and re-layouts  3.72 us (3%)
    pallas_call x12, Pallas kernels, whole(): pl.pallas_call(kernel, out_shape=out_shape, in_specs=[smem()] + [vmem()]...  19.2 us
    pallas_call x3, Pallas kernels, transforms(): pl.pallas_call(kernel, out_shape=out_shape, in_specs=[smem()] + [vmem()]...  18.2 us
    ppermute x4, waiting for transfers between devices, beside_cols(): wide = lax.ppermute(wide, 'cols', past_chip)  17 us
    ppermute x4, starting transfers between devices, beside_cols(): wide = lax.ppermute(wide, 'cols', past_chip)  11.1 us
    pallas_call x4, Pallas kernels, update(): pl.pallas_call(kernel, out_shape=jax.ShapeDtypeStruct(obj.shape, F32), in...  9 us
    ppermute x1, waiting for transfers between devices, per_device(): far[0] = lax.ppermute(mate[0], 'rows', outward)  6.2 us
    ppermute x1, waiting for transfers between devices, per_device(): lax.ppermute(mate_strip(0, meta, object_tiles, *ends, passing[0]), 'rows'...  6.13 us
    ppermute x1, waiting for transfers between devices, per_device(): far[1] = lax.ppermute(mate[1], 'rows', outward)  5.27 us
  transfers between devices with their start and end apart: 20, of which 8 were waited for; matrix products, arithmetic and copies ran while one was open for 0% of the time, Pallas kernels for 31%

commit v1 on v0

--- a/solution.py
+++ b/solution.py
@@ -325,7 +325,7 @@
             zg[part] = jnp.where(jnp.logical_and(live, show), x, 0.0)
 
 
-def second_kernel(meta, local, strip, psi, amp, la, lai, rb, rbi, g2, back, zg, v4, m4):
+def second_kernel(meta, local, strip, psi, amp, la, lai, rb, rbi, m4, zg, v4):
     for first in range(0, W, B):
         rows = pl.ds(first, B)
         o_re = window_rows(meta, local, strip, 0, first)
@@ -339,23 +339,27 @@
         factor = 1.0 - amp[rows, :].astype(F32) / jnp.sqrt(re * re + im * im + 1.0)
         put_left(v4, first, re * factor, im * factor, True)
     left_product(lai, v4, m4, True)
-    for first in range(0, W, B):
-        rows = pl.ds(first, B)
-        re, im = right_product(m4, rbi, first)
+    upper = meta[R0] < HALF
+    first = pl.multiple_of(jnp.where(upper, 0, W - B), B)
+    rows = pl.ds(first, B)
+    re, im = right_product(m4, rbi, first)
+    p_re, p_im = psi[0, rows, :], psi[1, rows, :]
+    below = rows_below(re.shape, first, meta[R0]).astype(jnp.int32)
+    leaves = jnp.logical_and(below + upper.astype(jnp.int32) == 1, meta[LIVE] > 0)
+    zg[0] = jnp.where(leaves, p_re * re + p_im * im, 0.0)
+    zg[1] = jnp.where(leaves, p_re * im - p_im * re, 0.0)
+
+
+def third_kernel(meta, mid, local, strip, psi, q, kern_re, kern_im, la, lai, rb, rbi, g2, g1, zg, v4, m4):
+    for first in range(0, W, B):
+        rows = pl.ds(first, B)
+        re, im = right_product(mid, rbi, first)
         p_re, p_im = psi[0, rows, :], psi[1, rows, :]
         g2[0, rows, :] = p_re * re + p_im * im
         g2[1, rows, :] = p_re * im - p_im * re
         o_re = window_rows(meta, local, strip, 0, first)
         o_im = window_rows(meta, local, strip, 1, first)
-        back[0, rows, :] = (o_re * re + o_im * im).astype(BF16)
-        back[1, rows, :] = (o_re * im - o_im * re).astype(BF16)
-    edge_rows(meta, g2, zg)
-
-
-def third_kernel(meta, back, q, kern_re, kern_im, la, lai, rb, rbi, g1, zg, v4, m4):
-    for first in range(0, W, B):
-        rows = pl.ds(first, B)
-        put_left(v4, first, back[0, rows, :], back[1, rows, :], False)
+        put_left(v4, first, o_re * re + o_im * im, o_re * im - o_im * re, False)
     left_product(la, v4, m4, False)
     for first in range(0, W, B):
         rows = pl.ds(first, B)
@@ -372,13 +376,13 @@
     edge_rows(meta, g1, zg)
 
 
-def transforms(kernel, name, out_shape, meta, *operands):
+def transforms(kernel, name, out_shape, meta, *operands, scratch=2):
     return pl.pallas_call(
         kernel,
         out_shape=out_shape,
         in_specs=[smem()] + [vmem()] * len(operands),
         out_specs=[vmem()] * len(out_shape),
-        scratch_shapes=[pltpu.VMEM((2 * W, 2 * W), BF16), pltpu.VMEM((2 * W, 2 * W), BF16)],
+        scratch_shapes=[pltpu.VMEM((2 * W, 2 * W), BF16)] * scratch,
         compiler_params=params(16),
         name=name,
     )(meta, *operands)
@@ -566,18 +570,21 @@
     tables = (la, lai, rb, rbi)
 
     (psi,) = transforms(first_kernel, "first", [WINDOW], meta, local[0], strip[0], q, *kernel, *tables)
-    g2, back, z2 = transforms(
+    mid, z2 = transforms(
         second_kernel,
         "second",
-        [WINDOW, jax.ShapeDtypeStruct((2, W, W), BF16), STRIP],
+        [jax.ShapeDtypeStruct((2 * W, 2 * W), BF16), STRIP],
         meta,
         local[1],
         strip[1],
         psi,
         amplitudes[0, 0, 0],
         *tables,
+        scratch=1,
     )
-    g1, z1 = transforms(third_kernel, "third", [WINDOW, STRIP], meta, back, q, *kernel, *tables)
+    g2, g1, z1 = transforms(
+        third_kernel, "third", [WINDOW, WINDOW, STRIP], meta, mid, local[1], strip[1], psi, q, *kernel, *tables
+    )
 
     mate, far, ends = [None, None], [None, None], [None, None]
     mate[1] = lax.ppermute(z2, "rows", mates)

time: 137 us -> 136 us (level)
  waiting for transfers between devices: 38.9 us -> 29.9 us
  starting transfers between devices: 40.1 us -> 46.6 us
    ppermute x4, starting transfers between devices: 11.1 us -> 19.2 us  [beside_cols(): wide = lax.ppermute(wide, 'cols', past_chip)]
    ppermute x4, waiting for transfers between devices: 17 us -> 10.7 us  [beside_cols(): wide = lax.ppermute(wide, 'cols', past_chip)]
    ppermute x1, starting transfers between devices: 3.67 us -> 1.91 us  [per_device(): far[1] = lax.ppermute(mate[1], 'rows', outward)]
    ppermute x1, waiting for transfers between devices: 6.2 us -> 4.83 us  [per_device(): far[0] = lax.ppermute(mate[0], 'rows', outward)]
  transfers between devices with their start and end apart: 20 -> 20, of which waited for: 8 -> 7; matrix products, arithmetic and copies ran while one was open for 0% -> 0% of each run, Pallas kernels for 31% -> 33%
where the time goes in v1:
time: 136 us; the launch traced here: 135 us
  Pallas kernels  53.3 us (39%)
  starting transfers between devices  46.6 us (34%)
  waiting for transfers between devices  29.9 us (22%)
  local copies, waits for them, and re-layouts  3.72 us (3%)
    pallas_call x12, Pallas kernels, whole(): pl.pallas_call(kernel, out_shape=out_shape, in_specs=[smem()] + [vmem()]...  19.2 us
    ppermute x4, starting transfers between devices, beside_cols(): wide = lax.ppermute(wide, 'cols', past_chip)  19.2 us
    pallas_call x3, Pallas kernels, transforms(): pl.pallas_call(kernel, out_shape=out_shape, in_specs=[smem()] + [vmem()]...  18.8 us
    ppermute x4, waiting for transfers between devices, beside_cols(): wide = lax.ppermute(wide, 'cols', past_chip)  10.7 us
    pallas_call x4, Pallas kernels, update(): pl.pallas_call(kernel, out_shape=jax.ShapeDtypeStruct(obj.shape, F32), in...  8.95 us
    ppermute x1, waiting for transfers between devices, per_device(): lax.ppermute(mate_strip(0, meta, object_tiles, *ends, passing[0]), 'rows'...  6.14 us
    pallas_call x2, Pallas kernels, edges(): pl.pallas_call(lambda *refs: edges_kernel(pieces, *refs), out_shape=[shap...  5.19 us
    ppermute x1, waiting for transfers between devices, per_device(): far[1] = lax.ppermute(mate[1], 'rows', outward)  4.97 us
  transfers between devices with their start and end apart: 20, of which 7 were waited for; matrix products, arithmetic and copies ran while one was open for 0% of the time, Pallas kernels for 33%

profile of v1, /device:TPU:19, one launch (start us, length us, event | category | flops | bytes accessed | tf_op | source)
XLA Modules:
  0.0 134.8 jit_solution(18080827109671021869)
XLA Ops:
  0.0 2.2 %edges.2 = (f32[2,2,256,128]{3,2,1,0:T(8,128)}, f32[2,2,256,128]{3,2,1,0:T(8,128)}) custom-call(s32[1]{0:T(128)} %bitcast.3.refs_0_.core, f32[2,2,768,768]{3,2,1,0:T(8,128)} %refs_2_.7), custom_call_target="tpu_custom_call" | custom-call | tf_op jit(solution)/shard_map/edges/pallas_call | solution.py:149
  2.3 1.7 %collective-permute-start = (s32[2]{0:T(128)S(1)}, s32[2]{0:T(128)S(1)}, u32[]{:S(2)}, u32[]{:S(2)}) collective-permute-start(s32[2]{0:T(128)S(1)} %bitcast.9), channel_id=1, source_target_pairs={{0,16},{16,0},{32,48},{48,32},{64,80},{80,64},{96,112},{112,96},{1... | collective-permute-start | bytes 32 | tf_op jit(solution)/shard_map/ppermute | solution.py:549
  4.0 2.0 %collective-permute-start.1 = (s32[2]{0:T(128)S(1)}, s32[2]{0:T(128)S(1)}, u32[]{:S(2)}, u32[]{:S(2)}) collective-permute-start(s32[2]{0:T(128)S(1)} %bitcast.10), channel_id=1, source_target_pairs={{16,32},{48,64},{80,96},{32,16},{64,48},{96,80},{17,33},{49,65},{8... | collective-permute-start | bytes 32 | tf_op jit(solution)/shard_map/ppermute | solution.py:549
  7.1 5.3 %collective-permute-start.3 = (f32[2,2,256,128]{3,2,1,0:T(8,128)}, f32[2,2,256,128]{3,2,1,0:T(8,128)S(1)}, u32[]{:S(2)}, u32[]{:S(2)}) collective-permute-start(f32[2,2,256,128]{3,2,1,0:T(8,128)} %get-tuple-element.64), channel_id=1, source_target_pairs={{1,2},{3,4},{5,6},{7,8},{9,10},{11,12},{13,14},{2,1},{4,3},{6,5},{... | collective-permute-start | bytes 1572872 | tf_op jit(solution)/shard_map/ppermute | solution.py:542
  12.4 3.0 %edges.3 = (f32[2,2,512,128]{3,2,1,0:T(8,128)}, f32[2,2,512,128]{3,2,1,0:T(8,128)}) custom-call(s32[1]{0:T(128)} %bitcast.3.refs_0_.core, f32[2,2,768,768]{3,2,1,0:T(8,128)} %refs_2_.7), custom_call_target="tpu_custom_call" | custom-call | tf_op jit(solution)/shard_map/edges/pallas_call | solution.py:149
  15.4 1.9 %collective-permute-start.6 = (f32[2,2,512,128]{3,2,1,0:T(8,128)}, f32[2,2,512,128]{3,2,1,0:T(8,128)S(1)}, u32[]{:S(2)}, u32[]{:S(2)}) collective-permute-start(f32[2,2,512,128]{3,2,1,0:T(8,128)} %get-tuple-element.73), channel_id=1, source_target_pairs={{1,2},{3,4},{5,6},{7,8},{9,10},{11,12},{13,14},{2,1},{4,3},{6,5},{... | collective-permute-start | bytes 3145736 | tf_op jit(solution)/shard_map/ppermute | solution.py:552
  18.0 3.7 %copy-done = f32[2,2,768,768]{3,2,1,0:T(8,128)S(1)} copy-done((f32[2,2,768,768]{3,2,1,0:T(8,128)S(1)}, f32[2,2,768,768]{3,2,1,0:T(8,128)}, u32[]{:S(2)}) %copy-start) | copy-done | bytes 9437208
  21.6 2.1 %phase.2 = (f32[512,512]{1,0:T(8,128)S(1)}, f32[512,512]{1,0:T(8,128)S(1)}) custom-call(s32[2]{0:T(128)S(1)} %bitcast.11, f32[512,512]{1,0:T(8,128)S(1)} %copy-done.2, f32[2,2,768,768]{3,2,1,0:T(8,128)S(1)} %copy-done), custom_call_target="tpu_custom_call" | custom-call | tf_op jit(solution)/shard_map/phase/pallas_call | solution.py:123
  25.9 10.5 %collective-permute-done.3.refs_3_ = f32[2,2,256,128]{3,2,1,0:T(8,128)S(1)} collective-permute-done((f32[2,2,256,128]{3,2,1,0:T(8,128)}, f32[2,2,256,128]{3,2,1,0:T(8,128)S(1)}, u32[]{:S(2)}, u32[]{:S(2)}) %collective-permute-start.3) | collective-permute-done | bytes 524320 | tf_op jit(solution)/shard_map/ppermute | solution.py:542
  37.0 2.3 %collective-permute-start.4 = (f32[2,128,512]{2,1,0:T(8,128)S(1)}, f32[2,128,512]{2,1,0:T(8,128)S(1)}, u32[]{:S(2)}, u32[]{:S(2)}) collective-permute-start(f32[2,128,512]{2,1,0:T(8,128)S(1)} %far_strip.2), channel_id=1, source_target_pairs={{32,0},{64,32},{96,64},{16,48},{48,80},{80,112},{33,1},{65,33},{97... | collective-permute-start | bytes 1572872 | tf_op jit(solution)/shard_map/ppermute | solution.py:561
  39.9 2.1 %collective-permute-start.7 = (f32[2,128,512]{2,1,0:T(8,128)S(1)}, f32[2,128,512]{2,1,0:T(8,128)S(1)}, u32[]{:S(2)}, u32[]{:S(2)}) collective-permute-start(f32[2,128,512]{2,1,0:T(8,128)S(1)} %far_strip.3), channel_id=1, source_target_pairs={{32,0},{64,32},{96,64},{16,48},{48,80},{80,112},{33,1},{65,33},{97... | collective-permute-start | bytes 1572872 | tf_op jit(solution)/shard_map/ppermute | solution.py:561
  42.0 3.9 %inverse_tables.1 = (bf16[512,1024]{1,0:T(8,128)(2,1)S(1)}, bf16[1024,512]{1,0:T(8,128)(2,1)S(1)}) custom-call(s32[9]{0:T(128)S(1)} %scalars.1.refs_0_.meta), custom_call_target="tpu_custom_call" | custom-call | tf_op jit(solution)/shard_map/inverse_tables/pallas_call | solution.py:123
  46.0 6.5 %forward_tables.1 = (bf16[512,1024]{1,0:T(8,128)(2,1)S(1)}, bf16[1024,512]{1,0:T(8,128)(2,1)S(1)}, f32[2,512,512]{2,1,0:T(8,128)S(1)}) custom-call(s32[9]{0:T(128)S(1)} %scalars.1.refs_0_.meta, f32[2,512,512]{2,1,0:T(8,128)S(1)} %copy-done.1), custom_call_target="tpu_custom_call" | custom-call | tf_op jit(solution)/shard_map/forward_tables/pallas_call | solution.py:123
  53.2 3.3 %collective-permute-start.9 = (f32[2,128,512]{2,1,0:T(8,128)S(1)}, f32[2,128,512]{2,1,0:T(8,128)S(1)}, u32[]{:S(2)}, u32[]{:S(2)}) collective-permute-start(f32[2,128,512]{2,1,0:T(8,128)S(1)} %mate_strip.3), channel_id=1, source_target_pairs={{0,16},{16,0},{32,48},{48,32},{64,80},{80,64},{96,112},{112,96},{1... | collective-permute-start | bytes 1572872 | tf_op jit(solution)/shard_map/ppermute | solution.py:566
  59.7 6.1 %collective-permute-done.9.strip = f32[2,128,512]{2,1,0:T(8,128)S(1)} collective-permute-done((f32[2,128,512]{2,1,0:T(8,128)S(1)}, f32[2,128,512]{2,1,0:T(8,128)S(1)}, u32[]{:S(2)}, u32[]{:S(2)}) %collective-permute-start.9) | collective-permute-done | bytes 524320 | tf_op jit(solution)/shard_map/ppermute | solution.py:566
  65.8 5.7 %first.1.psi = f32[2,512,512]{2,1,0:T(8,128)S(1)} custom-call(s32[9]{0:T(128)S(1)} %scalars.1.refs_0_.meta, f32[2,512,512]{2,1,0:T(8,128)S(1)} %local_window.3.local, f32[2,128,512]{2,1,0:T(8,128)S(1)} %collective-permute-done.9.strip, f32[2,512,512]{2,1,0:T(8,128)S(1)} %get-tuple-element.77.q, f32[512,512]{1,0:T(8,128)S(1)} %get-tuple-element.78.kern_re, ...), custom_call_target="tpu_custom_call" | custom-call | tf_op jit(solution)/shard_map/first/pallas_call | solution.py:380
  71.5 5.2 %second.1 = (bf16[1024,1024]{1,0:T(8,128)(2,1)S(1)}, f32[2,128,512]{2,1,0:T(8,128)S(1)}) custom-call(s32[9]{0:T(128)S(1)} %scalars.1.refs_0_.meta, f32[2,512,512]{2,1,0:T(8,128)S(1)} %local_window.2.local, f32[2,128,512]{2,1,0:T(8,128)S(1)} %collective-permute-done.8.strip, f32[2,512,512]{2,1,0:T(8,128)S(1)} %first.1.psi, bf16[512,512]{1,0:T(8,128)(2,1)S(1)} %bitcast.8, ...), custom_call_target="tpu_custom_call" | custom-call | tf_op jit(solution)/shard_map/second/pallas_call | solution.py:380
  77.5 7.9 %third.1 = (f32[2,512,512]{2,1,0:T(8,128)S(1)}, f32[2,512,512]{2,1,0:T(8,128)S(1)}, f32[2,128,512]{2,1,0:T(8,128)S(1)}) custom-call(s32[9]{0:T(128)S(1)} %scalars.1.refs_0_.meta, bf16[1024,1024]{1,0:T(8,128)(2,1)S(1)} %get-tuple-element.84.mid, f32[2,512,512]{2,1,0:T(8,128)S(1)} %local_window.2.local, f32[2,128,512]{2,1,0:T(8,128)S(1)} %collective-permute-done.8.strip, ...), custom_call_target="tpu_custom_call" | custom-call | tf_op jit(solution)/shard_map/third/pallas_call | solution.py:380
  87.4 3.2 %collective-permute-done.12.mate.refs_4_ = f32[2,128,512]{2,1,0:T(8,128)S(1)} collective-permute-done((f32[2,128,512]{2,1,0:T(8,128)S(1)}, f32[2,128,512]{2,1,0:T(8,128)S(1)}, u32[]{:S(2)}, u32[]{:S(2)}) %collective-permute-start.12) | collective-permute-done | bytes 524320 | tf_op jit(solution)/shard_map/ppermute | solution.py:590
  90.6 1.9 %collective-permute-start.17 = (f32[2,128,512]{2,1,0:T(8,128)S(1)}, f32[2,128,512]{2,1,0:T(8,128)S(1)}, u32[]{:S(2)}, u32[]{:S(2)}) collective-permute-start(f32[2,128,512]{2,1,0:T(8,128)S(1)} %collective-permute-done.12.mate.refs_4_), channel_id=1, source_target_pairs={{0,32},{32,64},{64,96},{48,16},{80,48},{112,80},{1,33},{33,65},{65... | collective-permute-start | bytes 1572872 | tf_op jit(solution)/shard_map/ppermute | solution.py:592
  92.5 4.1 %collective-permute-start.14 = (f32[2,2,512,128]{3,2,1,0:T(8,128)S(1)}, f32[2,2,512,128]{3,2,1,0:T(8,128)S(1)}, u32[]{:S(2)}, u32[]{:S(2)}) collective-permute-start(f32[2,2,512,128]{3,2,1,0:T(8,128)S(1)} %get-tuple-element.92), channel_id=1, source_target_pairs={{1,2},{3,4},{5,6},{7,8},{9,10},{11,12},{13,14},{2,1},{4,3},{6,5},{... | collective-permute-start | bytes 3145736 | tf_op jit(solution)/shard_map/ppermute | solution.py:542
  96.7 3.8 %collective-permute-start.11 = (f32[2,128,512]{2,1,0:T(8,128)S(1)}, f32[2,128,512]{2,1,0:T(8,128)S(1)}, u32[]{:S(2)}, u32[]{:S(2)}) collective-permute-start(f32[2,128,512]{2,1,0:T(8,128)S(1)} %collective-permute-done.10.mate.refs_4_), channel_id=1, source_target_pairs={{0,32},{32,64},{64,96},{48,16},{80,48},{112,80},{1,33},{33,65},{65... | collective-permute-start | bytes 1572872 | tf_op jit(solution)/shard_map/ppermute | solution.py:595
  100.5 5.0 %collective-permute-done.17.far.refs_5_ = f32[2,128,512]{2,1,0:T(8,128)S(1)} collective-permute-done((f32[2,128,512]{2,1,0:T(8,128)S(1)}, f32[2,128,512]{2,1,0:T(8,128)S(1)}, u32[]{:S(2)}, u32[]{:S(2)}) %collective-permute-start.17) | collective-permute-done | bytes 524320 | tf_op jit(solution)/shard_map/ppermute | solution.py:592
  106.2 2.4 %collective-permute-start.18 = (f32[2,256,128]{2,1,0:T(8,128)S(1)}, f32[2,256,128]{2,1,0:T(8,128)S(1)}, u32[]{:S(2)}, u32[]{:S(2)}) collective-permute-start(f32[2,256,128]{2,1,0:T(8,128)S(1)} %get-tuple-element.95), channel_id=1, source_target_pairs={{0,1},{1,0},{2,3},{3,2},{4,5},{5,4},{6,7},{7,6},{8,9},{9,8},{10,11... | collective-permute-start | bytes 786440 | tf_op jit(solution)/shard_map/ppermute | solution.py:543
  108.6 3.3 %collective-permute-start.19 = (f32[2,256,128]{2,1,0:T(8,128)S(1)}, f32[2,256,128]{2,1,0:T(8,128)S(1)}, u32[]{:S(2)}, u32[]{:S(2)}) collective-permute-start(f32[2,256,128]{2,1,0:T(8,128)S(1)} %get-tuple-element.96), channel_id=1, source_target_pairs={{1,2},{3,4},{5,6},{7,8},{9,10},{11,12},{13,14},{2,1},{4,3},{6,5},{... | collective-permute-start | bytes 786440 | tf_op jit(solution)/shard_map/ppermute | solution.py:542
  111.9 4.8 %collective-permute-done.11.far.refs_5_ = f32[2,128,512]{2,1,0:T(8,128)S(1)} collective-permute-done((f32[2,128,512]{2,1,0:T(8,128)S(1)}, f32[2,128,512]{2,1,0:T(8,128)S(1)}, u32[]{:S(2)}, u32[]{:S(2)}) %collective-permute-start.11) | collective-permute-done | bytes 524320 | tf_op jit(solution)/shard_map/ppermute | solution.py:595
  117.4 1.4 %collective-permute-start.15 = (f32[2,256,128]{2,1,0:T(8,128)S(1)}, f32[2,256,128]{2,1,0:T(8,128)S(1)}, u32[]{:S(2)}, u32[]{:S(2)}) collective-permute-start(f32[2,256,128]{2,1,0:T(8,128)S(1)} %get-tuple-element.93), channel_id=1, source_target_pairs={{0,1},{1,0},{2,3},{3,2},{4,5},{5,4},{6,7},{7,6},{8,9},{9,8},{10,11... | collective-permute-start | bytes 786440 | tf_op jit(solution)/shard_map/ppermute | solution.py:543
  118.8 6.5 %collective-permute-start.16 = (f32[2,256,128]{2,1,0:T(8,128)S(1)}, f32[2,256,128]{2,1,0:T(8,128)S(1)}, u32[]{:S(2)}, u32[]{:S(2)}) collective-permute-start(f32[2,256,128]{2,1,0:T(8,128)S(1)} %get-tuple-element.94), channel_id=1, source_target_pairs={{1,2},{3,4},{5,6},{7,8},{9,10},{11,12},{13,14},{2,1},{4,3},{6,5},{... | collective-permute-start | bytes 786440 | tf_op jit(solution)/shard_map/ppermute | solution.py:542
  125.4 2.5 %inner.2.refs_6_ = f32[2,2,768,768]{3,2,1,0:T(8,128)} custom-call(s32[9]{0:T(128)S(1)} %scalars.1.refs_0_.meta, f32[2]{0:T(128)S(1)} %copy-done.4, f32[2,2,768,768]{3,2,1,0:T(8,128)S(1)} %bitcast.7, f32[2,512,512]{2,1,0:T(8,128)S(1)} %get-tuple-element.88.g2.g.refs_3_, f32[2,128,512]{2,1,0:T(8,128)S(1)} %collective-permute-done.12.mate.refs_4_, ...), custom_call_target="tpu_custom_call" | custom-call | tf_op jit(solution)/shard_map/inner/pallas_call | solution.py:501
  127.9 2.5 %inner.3.refs_10_ = f32[2,2,768,768]{3,2,1,0:T(8,128)} custom-call(s32[9]{0:T(128)S(1)} %scalars.1.refs_0_.meta, f32[2]{0:T(128)S(1)} %copy-done.4, f32[2,2,768,768]{3,2,1,0:T(8,128)S(1)} %bitcast.7, f32[2,512,512]{2,1,0:T(8,128)S(1)} %get-tuple-element.85.g1.g.refs_3_, ...), custom_call_target="tpu_custom_call", output_to_operand_aliasing={{}: (6, {})} | custom-call | tf_op jit(solution)/shard_map/inner/pallas_call | solution.py:501
  130.4 2.0 %border.2.refs_10_ = f32[2,2,768,768]{3,2,1,0:T(8,128)} custom-call(s32[9]{0:T(128)S(1)} %scalars.1.refs_0_.meta, f32[2]{0:T(128)S(1)} %copy-done.4, f32[2,2,768,768]{3,2,1,0:T(8,128)S(1)} %bitcast.7, f32[2,512,512]{2,1,0:T(8,128)S(1)} %get-tuple-element.88.g2.g.refs_3_, ...), custom_call_target="tpu_custom_call", output_to_operand_aliasing={{}: (10, {})} | custom-call | tf_op jit(solution)/shard_map/border/pallas_call | solution.py:501
  132.6 2.0 %border.3 = f32[2,2,768,768]{3,2,1,0:T(8,128)} custom-call(s32[9]{0:T(128)S(1)} %scalars.1.refs_0_.meta, f32[2]{0:T(128)S(1)} %copy-done.4, f32[2,2,768,768]{3,2,1,0:T(8,128)S(1)} %bitcast.7, f32[2,512,512]{2,1,0:T(8,128)S(1)} %get-tuple-element.85.g1.g.refs_3_, ...), custom_call_target="tpu_custom_call", output_to_operand_aliasing={{}: (10, {})} | custom-call | tf_op jit(solution)/shard_map/border/pallas_call | solution.py:501
  (51 shorter events, 12.7 us)
Async XLA Ops:
  0.0 2.2 %copy-start.5 = (s32[1,1,1,2]{3,2,1,0:T(1,128)S(1)}, s32[1,1,1,2]{3,2,1,0:T(1,128)}, u32[]{:S(2)}) copy-start(s32[1,1,1,2]{3,2,1,0:T(1,128)} %param.11) | copy-start | bytes 28
  2.3 15.7 %copy-start.2 = (f32[512,512]{1,0:T(8,128)S(1)}, f32[512,512]{1,0:T(8,128)}, u32[]{:S(2)}) copy-start(f32[512,512]{1,0:T(8,128)} %phase.3) | copy-start | bytes 3145732
  2.3 21.5 %collective-permute-start = (s32[2]{0:T(128)S(1)}, s32[2]{0:T(128)S(1)}, u32[]{:S(2)}, u32[]{:S(2)}) collective-permute-start(s32[2]{0:T(128)S(1)} %bitcast.9), channel_id=1, source_target_pairs={{0,16},{16,0},{32,48},{48,32},{64,80},{80,64},{96,112},{112,96},{1... | collective-permute-start | bytes 32 | tf_op jit(solution)/shard_map/ppermute | solution.py:549
  4.0 19.8 %collective-permute-start.1 = (s32[2]{0:T(128)S(1)}, s32[2]{0:T(128)S(1)}, u32[]{:S(2)}, u32[]{:S(2)}) collective-permute-start(s32[2]{0:T(128)S(1)} %bitcast.10), channel_id=1, source_target_pairs={{16,32},{48,64},{80,96},{32,16},{64,48},{96,80},{17,33},{49,65},{8... | collective-permute-start | bytes 32 | tf_op jit(solution)/shard_map/ppermute | solution.py:549
  6.0 19.8 %collective-permute-start.2 = (f32[2,2,256,128]{3,2,1,0:T(8,128)}, f32[2,2,256,128]{3,2,1,0:T(8,128)S(1)}, u32[]{:S(2)}, u32[]{:S(2)}) collective-permute-start(f32[2,2,256,128]{3,2,1,0:T(8,128)} %get-tuple-element.63), channel_id=1, source_target_pairs={{0,1},{1,0},{2,3},{3,2},{4,5},{5,4},{6,7},{7,6},{8,9},{9,8},{10,11... | collective-permute-start | bytes 1572872 | tf_op jit(solution)/shard_map/ppermute | solution.py:543
  7.1 29.2 %collective-permute-start.3 = (f32[2,2,256,128]{3,2,1,0:T(8,128)}, f32[2,2,256,128]{3,2,1,0:T(8,128)S(1)}, u32[]{:S(2)}, u32[]{:S(2)}) collective-permute-start(f32[2,2,256,128]{3,2,1,0:T(8,128)} %get-tuple-element.64), channel_id=1, source_target_pairs={{1,2},{3,4},{5,6},{7,8},{9,10},{11,12},{13,14},{2,1},{4,3},{6,5},{... | collective-permute-start | bytes 1572872 | tf_op jit(solution)/shard_map/ppermute | solution.py:542
  15.4 37.1 %collective-permute-start.6 = (f32[2,2,512,128]{3,2,1,0:T(8,128)}, f32[2,2,512,128]{3,2,1,0:T(8,128)S(1)}, u32[]{:S(2)}, u32[]{:S(2)}) collective-permute-start(f32[2,2,512,128]{3,2,1,0:T(8,128)} %get-tuple-element.73), channel_id=1, source_target_pairs={{1,2},{3,4},{5,6},{7,8},{9,10},{11,12},{13,14},{2,1},{4,3},{6,5},{... | collective-permute-start | bytes 3145736 | tf_op jit(solution)/shard_map/ppermute | solution.py:552
  18.0 3.7 %copy-start = (f32[2,2,768,768]{3,2,1,0:T(8,128)S(1)}, f32[2,2,768,768]{3,2,1,0:T(8,128)}, u32[]{:S(2)}) copy-start(f32[2,2,768,768]{3,2,1,0:T(8,128)} %refs_2_.7) | copy-start | bytes 28311556
  21.6 3.3 %copy-start.6 = (f32[2,2,512,128]{3,2,1,0:T(8,128)S(1)}, f32[2,2,512,128]{3,2,1,0:T(8,128)}, u32[]{:S(2)}) copy-start(f32[2,2,512,128]{3,2,1,0:T(8,128)} %get-tuple-element.72) | copy-start | bytes 3145732
  25.0 27.5 %collective-permute-start.5 = (f32[2,2,512,128]{3,2,1,0:T(8,128)S(1)}, f32[2,2,512,128]{3,2,1,0:T(8,128)S(1)}, u32[]{:S(2)}, u32[]{:S(2)}) collective-permute-start(f32[2,2,512,128]{3,2,1,0:T(8,128)S(1)} %copy-done.6), channel_id=1, source_target_pairs={{0,1},{1,0},{2,3},{3,2},{4,5},{5,4},{6,7},{7,6},{8,9},{9,8},{10,11... | collective-permute-start | bytes 3145736 | tf_op jit(solution)/shard_map/ppermute | solution.py:557
  36.3 16.2 %slice-start = ((s8[9437184]{0:T(1024)(128)(4,1)}), s8[4194304]{0:T(1024)(128)(4,1)S(1)}, s32[]{:S(2)}) async-start(s8[9437184]{0:T(1024)(128)(4,1)} %bitcast.6), calls=%async_computation | async-start | bytes 8388608
  36.3 16.2 %slice-start.1 = ((s8[9437184]{0:T(1024)(128)(4,1)}), s8[4194304]{0:T(1024)(128)(4,1)S(1)}, s32[]{:S(2)}) async-start(s8[9437184]{0:T(1024)(128)(4,1)} %bitcast.6), calls=%async_computation.1 | async-start | bytes 8388608
  36.9 9.0 %copy-start.1 = (f32[2,512,512]{2,1,0:T(8,128)S(1)}, f32[2,512,512]{2,1,0:T(8,128)}, u32[]{:S(2)}) copy-start(f32[2,512,512]{2,1,0:T(8,128)} %probe.1) | copy-start | bytes 6291460
  37.0 15.6 %slice-start.2 = ((s8[9437184]{0:T(1024)(128)(4,1)}), s8[1048576]{0:T(1024)(128)(4,1)S(1)}, s32[]{:S(2)}) async-start(s8[9437184]{0:T(1024)(128)(4,1)} %bitcast.6), calls=%async_computation.2 | async-start | bytes 2097152
  37.0 15.5 %collective-permute-start.4 = (f32[2,128,512]{2,1,0:T(8,128)S(1)}, f32[2,128,512]{2,1,0:T(8,128)S(1)}, u32[]{:S(2)}, u32[]{:S(2)}) collective-permute-start(f32[2,128,512]{2,1,0:T(8,128)S(1)} %far_strip.2), channel_id=1, source_target_pairs={{32,0},{64,32},{96,64},{16,48},{48,80},{80,112},{33,1},{65,33},{97... | collective-permute-start | bytes 1572872 | tf_op jit(solution)/shard_map/ppermute | solution.py:561
  39.9 16.5 %collective-permute-start.7 = (f32[2,128,512]{2,1,0:T(8,128)S(1)}, f32[2,128,512]{2,1,0:T(8,128)S(1)}, u32[]{:S(2)}, u32[]{:S(2)}) collective-permute-start(f32[2,128,512]{2,1,0:T(8,128)S(1)} %far_strip.3), channel_id=1, source_target_pairs={{32,0},{64,32},{96,64},{16,48},{48,80},{80,112},{33,1},{65,33},{97... | collective-permute-start | bytes 1572872 | tf_op jit(solution)/shard_map/ppermute | solution.py:561
  53.2 12.6 %collective-permute-start.9 = (f32[2,128,512]{2,1,0:T(8,128)S(1)}, f32[2,128,512]{2,1,0:T(8,128)S(1)}, u32[]{:S(2)}, u32[]{:S(2)}) collective-permute-start(f32[2,128,512]{2,1,0:T(8,128)S(1)} %mate_strip.3), channel_id=1, source_target_pairs={{0,16},{16,0},{32,48},{48,32},{64,80},{80,64},{96,112},{112,96},{1... | collective-permute-start | bytes 1572872 | tf_op jit(solution)/shard_map/ppermute | solution.py:566
  57.1 14.4 %collective-permute-start.8 = (f32[2,128,512]{2,1,0:T(8,128)S(1)}, f32[2,128,512]{2,1,0:T(8,128)S(1)}, u32[]{:S(2)}, u32[]{:S(2)}) collective-permute-start(f32[2,128,512]{2,1,0:T(8,128)S(1)} %mate_strip.2), channel_id=1, source_target_pairs={{0,16},{16,0},{32,48},{48,32},{64,80},{80,64},{96,112},{112,96},{1... | collective-permute-start | bytes 1572872 | tf_op jit(solution)/shard_map/ppermute | solution.py:569
  59.6 11.9 %copy-start.3 = (bf16[1,1,1,512,512]{4,3,2,1,0:T(8,128)(2,1)S(1)}, bf16[1,1,1,512,512]{4,3,2,1,0:T(8,128)(2,1)}, u32[]{:S(2)}) copy-start(bf16[1,1,1,512,512]{4,3,2,1,0:T(8,128)(2,1)} %param.10) | copy-start | bytes 1572868
  76.8 13.8 %collective-permute-start.12 = (f32[2,128,512]{2,1,0:T(8,128)S(1)}, f32[2,128,512]{2,1,0:T(8,128)S(1)}, u32[]{:S(2)}, u32[]{:S(2)}) collective-permute-start(f32[2,128,512]{2,1,0:T(8,128)S(1)} %get-tuple-element.87), channel_id=1, source_target_pairs={{0,16},{16,0},{32,48},{48,32},{64,80},{80,64},{96,112},{112,96},{1... | collective-permute-start | bytes 1572872 | tf_op jit(solution)/shard_map/ppermute | solution.py:590
  85.4 11.3 %collective-permute-start.10 = (f32[2,128,512]{2,1,0:T(8,128)S(1)}, f32[2,128,512]{2,1,0:T(8,128)S(1)}, u32[]{:S(2)}, u32[]{:S(2)}) collective-permute-start(f32[2,128,512]{2,1,0:T(8,128)S(1)} %get-tuple-element.86), channel_id=1, source_target_pairs={{0,16},{16,0},{32,48},{48,32},{64,80},{80,64},{96,112},{112,96},{1... | collective-permute-start | bytes 1572872 | tf_op jit(solution)/shard_map/ppermute | solution.py:591
  90.6 39.7 %collective-permute-start.13 = (f32[2,2,512,128]{3,2,1,0:T(8,128)S(1)}, f32[2,2,512,128]{3,2,1,0:T(8,128)S(1)}, u32[]{:S(2)}, u32[]{:S(2)}) collective-permute-start(f32[2,2,512,128]{3,2,1,0:T(8,128)S(1)} %get-tuple-element.91), channel_id=1, source_target_pairs={{0,1},{1,0},{2,3},{3,2},{4,5},{5,4},{6,7},{7,6},{8,9},{9,8},{10,11... | collective-permute-start | bytes 3145736 | tf_op jit(solution)/shard_map/ppermute | solution.py:543
  90.6 14.9 %collective-permute-start.17 = (f32[2,128,512]{2,1,0:T(8,128)S(1)}, f32[2,128,512]{2,1,0:T(8,128)S(1)}, u32[]{:S(2)}, u32[]{:S(2)}) collective-permute-start(f32[2,128,512]{2,1,0:T(8,128)S(1)} %collective-permute-done.12.mate.refs_4_), channel_id=1, source_target_pairs={{0,32},{32,64},{64,96},{48,16},{80,48},{112,80},{1,33},{33,65},{65... | collective-permute-start | bytes 1572872 | tf_op jit(solution)/shard_map/ppermute | solution.py:592
  92.5 37.8 %collective-permute-start.14 = (f32[2,2,512,128]{3,2,1,0:T(8,128)S(1)}, f32[2,2,512,128]{3,2,1,0:T(8,128)S(1)}, u32[]{:S(2)}, u32[]{:S(2)}) collective-permute-start(f32[2,2,512,128]{3,2,1,0:T(8,128)S(1)} %get-tuple-element.92), channel_id=1, source_target_pairs={{1,2},{3,4},{5,6},{7,8},{9,10},{11,12},{13,14},{2,1},{4,3},{6,5},{... | collective-permute-start | bytes 3145736 | tf_op jit(solution)/shard_map/ppermute | solution.py:542
  96.7 20.0 %collective-permute-start.11 = (f32[2,128,512]{2,1,0:T(8,128)S(1)}, f32[2,128,512]{2,1,0:T(8,128)S(1)}, u32[]{:S(2)}, u32[]{:S(2)}) collective-permute-start(f32[2,128,512]{2,1,0:T(8,128)S(1)} %collective-permute-done.10.mate.refs_4_), channel_id=1, source_target_pairs={{0,32},{32,64},{64,96},{48,16},{80,48},{112,80},{1,33},{33,65},{65... | collective-permute-start | bytes 1572872 | tf_op jit(solution)/shard_map/ppermute | solution.py:595
  106.2 19.2 %copy-start.4 = (f32[2]{0:T(128)S(1)}, f32[2]{0:T(128)}, u32[]{:S(2)}) copy-start(f32[2]{0:T(128)} %refs_1_.22) | copy-start | bytes 28
  106.2 12.7 %collective-permute-start.18 = (f32[2,256,128]{2,1,0:T(8,128)S(1)}, f32[2,256,128]{2,1,0:T(8,128)S(1)}, u32[]{:S(2)}, u32[]{:S(2)}) collective-permute-start(f32[2,256,128]{2,1,0:T(8,128)S(1)} %get-tuple-element.95), channel_id=1, source_target_pairs={{0,1},{1,0},{2,3},{3,2},{4,5},{5,4},{6,7},{7,6},{8,9},{9,8},{10,11... | collective-permute-start | bytes 786440 | tf_op jit(solution)/shard_map/ppermute | solution.py:543
  108.6 21.8 %collective-permute-start.19 = (f32[2,256,128]{2,1,0:T(8,128)S(1)}, f32[2,256,128]{2,1,0:T(8,128)S(1)}, u32[]{:S(2)}, u32[]{:S(2)}) collective-permute-start(f32[2,256,128]{2,1,0:T(8,128)S(1)} %get-tuple-element.96), channel_id=1, source_target_pairs={{1,2},{3,4},{5,6},{7,8},{9,10},{11,12},{13,14},{2,1},{4,3},{6,5},{... | collective-permute-start | bytes 786440 | tf_op jit(solution)/shard_map/ppermute | solution.py:542
  117.4 15.0 %collective-permute-start.15 = (f32[2,256,128]{2,1,0:T(8,128)S(1)}, f32[2,256,128]{2,1,0:T(8,128)S(1)}, u32[]{:S(2)}, u32[]{:S(2)}) collective-permute-start(f32[2,256,128]{2,1,0:T(8,128)S(1)} %get-tuple-element.93), channel_id=1, source_target_pairs={{0,1},{1,0},{2,3},{3,2},{4,5},{5,4},{6,7},{7,6},{8,9},{9,8},{10,11... | collective-permute-start | bytes 786440 | tf_op jit(solution)/shard_map/ppermute | solution.py:543
  118.8 13.8 %collective-permute-start.16 = (f32[2,256,128]{2,1,0:T(8,128)S(1)}, f32[2,256,128]{2,1,0:T(8,128)S(1)}, u32[]{:S(2)}, u32[]{:S(2)}) collective-permute-start(f32[2,256,128]{2,1,0:T(8,128)S(1)} %get-tuple-element.94), channel_id=1, source_target_pairs={{1,2},{3,4},{5,6},{7,8},{9,10},{11,12},{13,14},{2,1},{4,3},{6,5},{... | collective-permute-start | bytes 786440 | tf_op jit(solution)/shard_map/ppermute | solution.py:542

commit v2 on v1

--- a/solution.py
+++ b/solution.py
@@ -556,12 +556,14 @@
     middle_near, _ = after(sent[0], meta)
     middle = lax.ppermute(middle_near, "cols", at_chip), middle_wide
 
+    la, rb, q = whole(forward_kernel, "forward_tables", [LEFT, RIGHT, WINDOW], meta, probe)
+    *ends, la, rb, q = after(*ends, la, rb, q)
+
     for s in range(2):
         far[s] = far_strip(s, meta, object_tiles, *ends)
         passing[s] = lax.ppermute(far[s], "rows", inward)
     third, _ = after(meta, far[1])
     lai, rbi = whole(inverse_kernel, "inverse_tables", [LEFT, RIGHT], third)
-    la, rb, q = whole(forward_kernel, "forward_tables", [LEFT, RIGHT, WINDOW], third, probe)
     passing[0], la, rb, q, lai, rbi, *middle = after(passing[0], la, rb, q, lai, rbi, *middle)
     strip[0] = lax.ppermute(mate_strip(0, meta, object_tiles, *ends, passing[0]), "rows", mates)
     local[0] = local_window(0, meta, object_tiles, *ends, *middle)

time: 136 us -> 144 us (1.059)
  the two profiles are of different devices: /device:TPU:19 before, /device:TPU:37 now
where the time goes in v2:
time: 144 us
  Pallas kernels  53.5 us (37%)
  waiting for transfers between devices  50.9 us (35%)
  starting transfers between devices  34.5 us (24%)
  local copies, waits for them, and re-layouts  3.72 us (3%)
    pallas_call x12, Pallas kernels, whole(): pl.pallas_call(kernel, out_shape=out_shape, in_specs=[smem()] + [vmem()]...  19.2 us
    pallas_call x3, Pallas kernels, transforms(): pl.pallas_call(kernel, out_shape=out_shape, in_specs=[smem()] + [vmem()]...  18.8 us
    ppermute x2, waiting for transfers between devices, per_device(): passing[s] = lax.ppermute(far[s], 'rows', inward)  15.2 us
    ppermute x4, starting transfers between devices, beside_cols(): wide = lax.ppermute(wide, 'cols', past_chip)  13.9 us
    ppermute x1, waiting for transfers between devices, per_device(): mate[0] = lax.ppermute(z1, 'rows', mates)  13.9 us
    ppermute x1, waiting for transfers between devices, per_device(): far[0] = lax.ppermute(mate[0], 'rows', outward)  9.95 us
    pallas_call x4, Pallas kernels, update(): pl.pallas_call(kernel, out_shape=jax.ShapeDtypeStruct(obj.shape, F32), in...  9.05 us
    pallas_call x2, Pallas kernels, edges(): pl.pallas_call(lambda *refs: edges_kernel(pieces, *refs), out_shape=[shap...  5.34 us
  transfers between devices with their start and end apart: 20, of which 8 were waited for; matrix products, arithmetic and copies ran while one was open for 0% of the time, Pallas kernels for 31%

profile of v2, /device:TPU:37, one launch (start us, length us, event | category | flops | bytes accessed | tf_op | source)
XLA Modules:
  0.0 143.9 jit_solution(13288555456306233898)
XLA Ops:
  0.0 2.2 %edges.2 = (f32[2,2,256,128]{3,2,1,0:T(8,128)}, f32[2,2,256,128]{3,2,1,0:T(8,128)}) custom-call(s32[1]{0:T(128)} %bitcast.3.refs_0_.core, f32[2,2,768,768]{3,2,1,0:T(8,128)} %refs_2_.7), custom_call_target="tpu_custom_call" | custom-call | tf_op jit(solution)/shard_map/edges/pallas_call | solution.py:149
  2.4 4.0 %collective-permute-start.1 = (s32[2]{0:T(128)S(1)}, s32[2]{0:T(128)S(1)}, u32[]{:S(2)}, u32[]{:S(2)}) collective-permute-start(s32[2]{0:T(128)S(1)} %bitcast.10), channel_id=1, source_target_pairs={{16,32},{48,64},{80,96},{32,16},{64,48},{96,80},{17,33},{49,65},{8... | collective-permute-start | bytes 32 | tf_op jit(solution)/shard_map/ppermute | solution.py:549
  6.3 1.3 collective-permute-start.2
  7.7 4.5 %collective-permute-start.3 = (f32[2,2,256,128]{3,2,1,0:T(8,128)}, f32[2,2,256,128]{3,2,1,0:T(8,128)S(1)}, u32[]{:S(2)}, u32[]{:S(2)}) collective-permute-start(f32[2,2,256,128]{3,2,1,0:T(8,128)} %get-tuple-element.69), channel_id=1, source_target_pairs={{1,2},{3,4},{5,6},{7,8},{9,10},{11,12},{13,14},{2,1},{4,3},{6,5},{... | collective-permute-start | bytes 1572872 | tf_op jit(solution)/shard_map/ppermute | solution.py:542
  12.2 3.1 %edges.3 = (f32[2,2,512,128]{3,2,1,0:T(8,128)}, f32[2,2,512,128]{3,2,1,0:T(8,128)}) custom-call(s32[1]{0:T(128)} %bitcast.3.refs_0_.core, f32[2,2,768,768]{3,2,1,0:T(8,128)} %refs_2_.7), custom_call_target="tpu_custom_call" | custom-call | tf_op jit(solution)/shard_map/edges/pallas_call | solution.py:149
  15.3 2.6 %collective-permute-start.6 = (f32[2,2,512,128]{3,2,1,0:T(8,128)}, f32[2,2,512,128]{3,2,1,0:T(8,128)S(1)}, u32[]{:S(2)}, u32[]{:S(2)}) collective-permute-start(f32[2,2,512,128]{3,2,1,0:T(8,128)} %get-tuple-element.83), channel_id=1, source_target_pairs={{1,2},{3,4},{5,6},{7,8},{9,10},{11,12},{13,14},{2,1},{4,3},{6,5},{... | collective-permute-start | bytes 3145736 | tf_op jit(solution)/shard_map/ppermute | solution.py:552
  18.5 3.7 %copy-done = f32[2,2,768,768]{3,2,1,0:T(8,128)S(1)} copy-done((f32[2,2,768,768]{3,2,1,0:T(8,128)S(1)}, f32[2,2,768,768]{3,2,1,0:T(8,128)}, u32[]{:S(2)}) %copy-start) | copy-done | bytes 9437208
  22.2 2.1 %phase.2 = (f32[512,512]{1,0:T(8,128)S(1)}, f32[512,512]{1,0:T(8,128)S(1)}) custom-call(s32[2]{0:T(128)S(1)} %bitcast.11, f32[512,512]{1,0:T(8,128)S(1)} %copy-done.2, f32[2,2,768,768]{3,2,1,0:T(8,128)S(1)} %copy-done), custom_call_target="tpu_custom_call" | custom-call | tf_op jit(solution)/shard_map/phase/pallas_call | solution.py:123
  25.7 6.5 %forward_tables.1 = (bf16[512,1024]{1,0:T(8,128)(2,1)S(1)}, bf16[1024,512]{1,0:T(8,128)(2,1)S(1)}, f32[2,512,512]{2,1,0:T(8,128)S(1)}) custom-call(s32[9]{0:T(128)S(1)} %scalars.1.meta.refs_0_, f32[2,512,512]{2,1,0:T(8,128)S(1)} %copy-done.1), custom_call_target="tpu_custom_call" | custom-call | tf_op jit(solution)/shard_map/forward_tables/pallas_call | solution.py:123
  32.2 3.3 %collective-permute-done.3.refs_3_ = f32[2,2,256,128]{3,2,1,0:T(8,128)S(1)} collective-permute-done((f32[2,2,256,128]{3,2,1,0:T(8,128)}, f32[2,2,256,128]{3,2,1,0:T(8,128)S(1)}, u32[]{:S(2)}, u32[]{:S(2)}) %collective-permute-start.3) | collective-permute-done | bytes 524320 | tf_op jit(solution)/shard_map/ppermute | solution.py:542
  36.1 1.9 %collective-permute-start.4 = (f32[2,128,512]{2,1,0:T(8,128)S(1)}, f32[2,128,512]{2,1,0:T(8,128)S(1)}, u32[]{:S(2)}, u32[]{:S(2)}) collective-permute-start(f32[2,128,512]{2,1,0:T(8,128)S(1)} %far_strip.2), channel_id=1, source_target_pairs={{32,0},{64,32},{96,64},{16,48},{48,80},{80,112},{33,1},{65,33},{97... | collective-permute-start | bytes 1572872 | tf_op jit(solution)/shard_map/ppermute | solution.py:564
  38.6 2.1 %collective-permute-start.7 = (f32[2,128,512]{2,1,0:T(8,128)S(1)}, f32[2,128,512]{2,1,0:T(8,128)S(1)}, u32[]{:S(2)}, u32[]{:S(2)}) collective-permute-start(f32[2,128,512]{2,1,0:T(8,128)S(1)} %far_strip.3), channel_id=1, source_target_pairs={{32,0},{64,32},{96,64},{16,48},{48,80},{80,112},{33,1},{65,33},{97... | collective-permute-start | bytes 1572872 | tf_op jit(solution)/shard_map/ppermute | solution.py:564
  40.7 3.9 %inverse_tables.1 = (bf16[512,1024]{1,0:T(8,128)(2,1)S(1)}, bf16[1024,512]{1,0:T(8,128)(2,1)S(1)}) custom-call(s32[9]{0:T(128)S(1)} %scalars.1.meta.refs_0_), custom_call_target="tpu_custom_call" | custom-call | tf_op jit(solution)/shard_map/inverse_tables/pallas_call | solution.py:123
  44.6 7.3 %collective-permute-done.4.refs_4_ = f32[2,128,512]{2,1,0:T(8,128)S(1)} collective-permute-done((f32[2,128,512]{2,1,0:T(8,128)S(1)}, f32[2,128,512]{2,1,0:T(8,128)S(1)}, u32[]{:S(2)}, u32[]{:S(2)}) %collective-permute-start.4) | collective-permute-done | bytes 524320 | tf_op jit(solution)/shard_map/ppermute | solution.py:564
  52.7 7.8 %collective-permute-done.7.refs_4_ = f32[2,128,512]{2,1,0:T(8,128)S(1)} collective-permute-done((f32[2,128,512]{2,1,0:T(8,128)S(1)}, f32[2,128,512]{2,1,0:T(8,128)S(1)}, u32[]{:S(2)}, u32[]{:S(2)}) %collective-permute-start.7) | collective-permute-done | bytes 524320 | tf_op jit(solution)/shard_map/ppermute | solution.py:564
  63.2 5.7 %first.1.psi = f32[2,512,512]{2,1,0:T(8,128)S(1)} custom-call(s32[9]{0:T(128)S(1)} %scalars.1.meta.refs_0_, f32[2,512,512]{2,1,0:T(8,128)S(1)} %local_window.3.local, f32[2,128,512]{2,1,0:T(8,128)S(1)} %collective-permute-done.9.strip, f32[2,512,512]{2,1,0:T(8,128)S(1)} %get-tuple-element.87.q, f32[512,512]{1,0:T(8,128)S(1)} %get-tuple-element.88.kern_re, ...), custom_call_target="tpu_custom_call" | custom-call | tf_op jit(solution)/shard_map/first/pallas_call | solution.py:380
  68.9 4.8 %collective-permute-done.8.strip = f32[2,128,512]{2,1,0:T(8,128)S(1)} collective-permute-done((f32[2,128,512]{2,1,0:T(8,128)S(1)}, f32[2,128,512]{2,1,0:T(8,128)S(1)}, u32[]{:S(2)}, u32[]{:S(2)}) %collective-permute-start.8) | collective-permute-done | bytes 524320 | tf_op jit(solution)/shard_map/ppermute | solution.py:571
  73.7 5.2 %second.1 = (bf16[1024,1024]{1,0:T(8,128)(2,1)S(1)}, f32[2,128,512]{2,1,0:T(8,128)S(1)}) custom-call(s32[9]{0:T(128)S(1)} %scalars.1.meta.refs_0_, f32[2,512,512]{2,1,0:T(8,128)S(1)} %local_window.2.local, f32[2,128,512]{2,1,0:T(8,128)S(1)} %collective-permute-done.8.strip, f32[2,512,512]{2,1,0:T(8,128)S(1)} %first.1.psi, bf16[512,512]{1,0:T(8,128)(2,1)S(1)} %bitcast.8, ...), custom_call_target="tpu_custom_call" | custom-call | tf_op jit(solution)/shard_map/second/pallas_call | solution.py:380
  79.3 7.9 %third.1 = (f32[2,512,512]{2,1,0:T(8,128)S(1)}, f32[2,512,512]{2,1,0:T(8,128)S(1)}, f32[2,128,512]{2,1,0:T(8,128)S(1)}) custom-call(s32[9]{0:T(128)S(1)} %scalars.1.meta.refs_0_, bf16[1024,1024]{1,0:T(8,128)(2,1)S(1)} %get-tuple-element.94.mid, f32[2,512,512]{2,1,0:T(8,128)S(1)} %local_window.2.local, f32[2,128,512]{2,1,0:T(8,128)S(1)} %collective-permute-done.8.strip, ...), custom_call_target="tpu_custom_call" | custom-call | tf_op jit(solution)/shard_map/third/pallas_call | solution.py:380
  87.2 1.5 %collective-permute-start.10 = (f32[2,128,512]{2,1,0:T(8,128)S(1)}, f32[2,128,512]{2,1,0:T(8,128)S(1)}, u32[]{:S(2)}, u32[]{:S(2)}) collective-permute-start(f32[2,128,512]{2,1,0:T(8,128)S(1)} %get-tuple-element.96), channel_id=1, source_target_pairs={{0,16},{16,0},{32,48},{48,32},{64,80},{80,64},{96,112},{112,96},{1... | collective-permute-start | bytes 1572872 | tf_op jit(solution)/shard_map/ppermute | solution.py:593
  89.6 3.7 %collective-permute-done.12.mate.refs_4_ = f32[2,128,512]{2,1,0:T(8,128)S(1)} collective-permute-done((f32[2,128,512]{2,1,0:T(8,128)S(1)}, f32[2,128,512]{2,1,0:T(8,128)S(1)}, u32[]{:S(2)}, u32[]{:S(2)}) %collective-permute-start.12) | collective-permute-done | bytes 524320 | tf_op jit(solution)/shard_map/ppermute | solution.py:592
  93.4 2.6 %collective-permute-start.17 = (f32[2,128,512]{2,1,0:T(8,128)S(1)}, f32[2,128,512]{2,1,0:T(8,128)S(1)}, u32[]{:S(2)}, u32[]{:S(2)}) collective-permute-start(f32[2,128,512]{2,1,0:T(8,128)S(1)} %collective-permute-done.12.mate.refs_4_), channel_id=1, source_target_pairs={{0,32},{32,64},{64,96},{48,16},{80,48},{112,80},{1,33},{33,65},{65... | collective-permute-start | bytes 1572872 | tf_op jit(solution)/shard_map/ppermute | solution.py:594
  96.0 5.6 %collective-permute-start.14 = (f32[2,2,512,128]{3,2,1,0:T(8,128)S(1)}, f32[2,2,512,128]{3,2,1,0:T(8,128)S(1)}, u32[]{:S(2)}, u32[]{:S(2)}) collective-permute-start(f32[2,2,512,128]{3,2,1,0:T(8,128)S(1)} %get-tuple-element.102), channel_id=1, source_target_pairs={{1,2},{3,4},{5,6},{7,8},{9,10},{11,12},{13,14},{2,1},{4,3},{6,5},{... | collective-permute-start | bytes 3145736 | tf_op jit(solution)/shard_map/ppermute | solution.py:542
  101.7 13.9 %collective-permute-done.10.mate.refs_4_ = f32[2,128,512]{2,1,0:T(8,128)S(1)} collective-permute-done((f32[2,128,512]{2,1,0:T(8,128)S(1)}, f32[2,128,512]{2,1,0:T(8,128)S(1)}, u32[]{:S(2)}, u32[]{:S(2)}) %collective-permute-start.10) | collective-permute-done | bytes 524320 | tf_op jit(solution)/shard_map/ppermute | solution.py:593
  115.5 1.9 %collective-permute-start.11 = (f32[2,128,512]{2,1,0:T(8,128)S(1)}, f32[2,128,512]{2,1,0:T(8,128)S(1)}, u32[]{:S(2)}, u32[]{:S(2)}) collective-permute-start(f32[2,128,512]{2,1,0:T(8,128)S(1)} %collective-permute-done.10.mate.refs_4_), channel_id=1, source_target_pairs={{0,32},{32,64},{64,96},{48,16},{80,48},{112,80},{1,33},{33,65},{65... | collective-permute-start | bytes 1572872 | tf_op jit(solution)/shard_map/ppermute | solution.py:597
  118.6 1.9 %collective-permute-start.19 = (f32[2,256,128]{2,1,0:T(8,128)S(1)}, f32[2,256,128]{2,1,0:T(8,128)S(1)}, u32[]{:S(2)}, u32[]{:S(2)}) collective-permute-start(f32[2,256,128]{2,1,0:T(8,128)S(1)} %get-tuple-element.106), channel_id=1, source_target_pairs={{1,2},{3,4},{5,6},{7,8},{9,10},{11,12},{13,14},{2,1},{4,3},{6,5},{... | collective-permute-start | bytes 786440 | tf_op jit(solution)/shard_map/ppermute | solution.py:542
  120.6 10.0 %collective-permute-done.11.far.refs_5_ = f32[2,128,512]{2,1,0:T(8,128)S(1)} collective-permute-done((f32[2,128,512]{2,1,0:T(8,128)S(1)}, f32[2,128,512]{2,1,0:T(8,128)S(1)}, u32[]{:S(2)}, u32[]{:S(2)}) %collective-permute-start.11) | collective-permute-done | bytes 524320 | tf_op jit(solution)/shard_map/ppermute | solution.py:597
  132.5 1.9 %collective-permute-start.16 = (f32[2,256,128]{2,1,0:T(8,128)S(1)}, f32[2,256,128]{2,1,0:T(8,128)S(1)}, u32[]{:S(2)}, u32[]{:S(2)}) collective-permute-start(f32[2,256,128]{2,1,0:T(8,128)S(1)} %get-tuple-element.104), channel_id=1, source_target_pairs={{1,2},{3,4},{5,6},{7,8},{9,10},{11,12},{13,14},{2,1},{4,3},{6,5},{... | collective-permute-start | bytes 786440 | tf_op jit(solution)/shard_map/ppermute | solution.py:542
  134.5 2.5 %inner.2.refs_6_ = f32[2,2,768,768]{3,2,1,0:T(8,128)} custom-call(s32[9]{0:T(128)S(1)} %scalars.1.meta.refs_0_, f32[2]{0:T(128)S(1)} %copy-done.4, f32[2,2,768,768]{3,2,1,0:T(8,128)S(1)} %bitcast.7, f32[2,512,512]{2,1,0:T(8,128)S(1)} %get-tuple-element.98.g2.g.refs_3_, f32[2,128,512]{2,1,0:T(8,128)S(1)} %collective-permute-done.12.mate.refs_4_, ...), custom_call_target="tpu_custom_call" | custom-call | tf_op jit(solution)/shard_map/inner/pallas_call | solution.py:501
  137.0 2.5 %inner.3.refs_10_ = f32[2,2,768,768]{3,2,1,0:T(8,128)} custom-call(s32[9]{0:T(128)S(1)} %scalars.1.meta.refs_0_, f32[2]{0:T(128)S(1)} %copy-done.4, f32[2,2,768,768]{3,2,1,0:T(8,128)S(1)} %bitcast.7, f32[2,512,512]{2,1,0:T(8,128)S(1)} %get-tuple-element.95.g1.g.refs_3_, ...), custom_call_target="tpu_custom_call", output_to_operand_aliasing={{}: (6, {})} | custom-call | tf_op jit(solution)/shard_map/inner/pallas_call | solution.py:501
  139.5 2.0 %border.2.refs_10_ = f32[2,2,768,768]{3,2,1,0:T(8,128)} custom-call(s32[9]{0:T(128)S(1)} %scalars.1.meta.refs_0_, f32[2]{0:T(128)S(1)} %copy-done.4, f32[2,2,768,768]{3,2,1,0:T(8,128)S(1)} %bitcast.7, f32[2,512,512]{2,1,0:T(8,128)S(1)} %get-tuple-element.98.g2.g.refs_3_, ...), custom_call_target="tpu_custom_call", output_to_operand_aliasing={{}: (10, {})} | custom-call | tf_op jit(solution)/shard_map/border/pallas_call | solution.py:501
  141.7 2.0 %border.3 = f32[2,2,768,768]{3,2,1,0:T(8,128)} custom-call(s32[9]{0:T(128)S(1)} %scalars.1.meta.refs_0_, f32[2]{0:T(128)S(1)} %copy-done.4, f32[2,2,768,768]{3,2,1,0:T(8,128)S(1)} %bitcast.7, f32[2,512,512]{2,1,0:T(8,128)S(1)} %get-tuple-element.95.g1.g.refs_3_, ...), custom_call_target="tpu_custom_call", output_to_operand_aliasing={{}: (10, {})} | custom-call | tf_op jit(solution)/shard_map/border/pallas_call | solution.py:501
  (51 shorter events, 10.7 us)
Async XLA Ops:
  0.0 2.2 %copy-start.5 = (s32[1,1,1,2]{3,2,1,0:T(1,128)S(1)}, s32[1,1,1,2]{3,2,1,0:T(1,128)}, u32[]{:S(2)}) copy-start(s32[1,1,1,2]{3,2,1,0:T(1,128)} %param.11) | copy-start | bytes 28
  2.3 16.3 %copy-start.2 = (f32[512,512]{1,0:T(8,128)S(1)}, f32[512,512]{1,0:T(8,128)}, u32[]{:S(2)}) copy-start(f32[512,512]{1,0:T(8,128)} %phase.3) | copy-start | bytes 3145732
  2.3 22.1 %collective-permute-start = (s32[2]{0:T(128)S(1)}, s32[2]{0:T(128)S(1)}, u32[]{:S(2)}, u32[]{:S(2)}) collective-permute-start(s32[2]{0:T(128)S(1)} %bitcast.9), channel_id=1, source_target_pairs={{0,16},{16,0},{32,48},{48,32},{64,80},{80,64},{96,112},{112,96},{1... | collective-permute-start | bytes 32 | tf_op jit(solution)/shard_map/ppermute | solution.py:549
  2.4 22.0 %collective-permute-start.1 = (s32[2]{0:T(128)S(1)}, s32[2]{0:T(128)S(1)}, u32[]{:S(2)}, u32[]{:S(2)}) collective-permute-start(s32[2]{0:T(128)S(1)} %bitcast.10), channel_id=1, source_target_pairs={{16,32},{48,64},{80,96},{32,16},{64,48},{96,80},{17,33},{49,65},{8... | collective-permute-start | bytes 32 | tf_op jit(solution)/shard_map/ppermute | solution.py:549
  6.3 25.8 %collective-permute-start.2 = (f32[2,2,256,128]{3,2,1,0:T(8,128)}, f32[2,2,256,128]{3,2,1,0:T(8,128)S(1)}, u32[]{:S(2)}, u32[]{:S(2)}) collective-permute-start(f32[2,2,256,128]{3,2,1,0:T(8,128)} %get-tuple-element.68), channel_id=1, source_target_pairs={{0,1},{1,0},{2,3},{3,2},{4,5},{5,4},{6,7},{7,6},{8,9},{9,8},{10,11... | collective-permute-start | bytes 1572872 | tf_op jit(solution)/shard_map/ppermute | solution.py:543
  7.7 27.8 %collective-permute-start.3 = (f32[2,2,256,128]{3,2,1,0:T(8,128)}, f32[2,2,256,128]{3,2,1,0:T(8,128)S(1)}, u32[]{:S(2)}, u32[]{:S(2)}) collective-permute-start(f32[2,2,256,128]{3,2,1,0:T(8,128)} %get-tuple-element.69), channel_id=1, source_target_pairs={{1,2},{3,4},{5,6},{7,8},{9,10},{11,12},{13,14},{2,1},{4,3},{6,5},{... | collective-permute-start | bytes 1572872 | tf_op jit(solution)/shard_map/ppermute | solution.py:542
  12.2 23.3 %slice-start = ((s8[9437184]{0:T(1024)(128)(4,1)}), s8[1048576]{0:T(1024)(128)(4,1)S(1)}, s32[]{:S(2)}) async-start(s8[9437184]{0:T(1024)(128)(4,1)} %bitcast.6), calls=%async_computation | async-start | bytes 2097152
  12.2 23.3 %slice-start.1 = ((s8[9437184]{0:T(1024)(128)(4,1)}), s8[4194304]{0:T(1024)(128)(4,1)S(1)}, s32[]{:S(2)}) async-start(s8[9437184]{0:T(1024)(128)(4,1)} %bitcast.6), calls=%async_computation.1 | async-start | bytes 8388608
  15.3 36.7 %collective-permute-start.6 = (f32[2,2,512,128]{3,2,1,0:T(8,128)}, f32[2,2,512,128]{3,2,1,0:T(8,128)S(1)}, u32[]{:S(2)}, u32[]{:S(2)}) collective-permute-start(f32[2,2,512,128]{3,2,1,0:T(8,128)} %get-tuple-element.83), channel_id=1, source_target_pairs={{1,2},{3,4},{5,6},{7,8},{9,10},{11,12},{13,14},{2,1},{4,3},{6,5},{... | collective-permute-start | bytes 3145736 | tf_op jit(solution)/shard_map/ppermute | solution.py:552
  18.5 3.7 %copy-start = (f32[2,2,768,768]{3,2,1,0:T(8,128)S(1)}, f32[2,2,768,768]{3,2,1,0:T(8,128)}, u32[]{:S(2)}) copy-start(f32[2,2,768,768]{3,2,1,0:T(8,128)} %refs_2_.7) | copy-start | bytes 28311556
  22.2 3.3 %copy-start.6 = (f32[2,2,512,128]{3,2,1,0:T(8,128)S(1)}, f32[2,2,512,128]{3,2,1,0:T(8,128)}, u32[]{:S(2)}) copy-start(f32[2,2,512,128]{3,2,1,0:T(8,128)} %get-tuple-element.82) | copy-start | bytes 3145732
  22.2 3.4 %copy-start.1 = (f32[2,512,512]{2,1,0:T(8,128)S(1)}, f32[2,512,512]{2,1,0:T(8,128)}, u32[]{:S(2)}) copy-start(f32[2,512,512]{2,1,0:T(8,128)} %probe.1) | copy-start | bytes 6291460
  22.2 13.2 %slice-start.2 = ((s8[9437184]{0:T(1024)(128)(4,1)}), s8[4194304]{0:T(1024)(128)(4,1)S(1)}, s32[]{:S(2)}) async-start(s8[9437184]{0:T(1024)(128)(4,1)} %bitcast.6), calls=%async_computation.2 | async-start | bytes 8388608
  25.6 26.4 %collective-permute-start.5 = (f32[2,2,512,128]{3,2,1,0:T(8,128)S(1)}, f32[2,2,512,128]{3,2,1,0:T(8,128)S(1)}, u32[]{:S(2)}, u32[]{:S(2)}) collective-permute-start(f32[2,2,512,128]{3,2,1,0:T(8,128)S(1)} %copy-done.6), channel_id=1, source_target_pairs={{0,1},{1,0},{2,3},{3,2},{4,5},{5,4},{6,7},{7,6},{8,9},{9,8},{10,11... | collective-permute-start | bytes 3145736 | tf_op jit(solution)/shard_map/ppermute | solution.py:557
  36.1 15.9 %collective-permute-start.4 = (f32[2,128,512]{2,1,0:T(8,128)S(1)}, f32[2,128,512]{2,1,0:T(8,128)S(1)}, u32[]{:S(2)}, u32[]{:S(2)}) collective-permute-start(f32[2,128,512]{2,1,0:T(8,128)S(1)} %far_strip.2), channel_id=1, source_target_pairs={{32,0},{64,32},{96,64},{16,48},{48,80},{80,112},{33,1},{65,33},{97... | collective-permute-start | bytes 1572872 | tf_op jit(solution)/shard_map/ppermute | solution.py:564
  38.6 22.0 %collective-permute-start.7 = (f32[2,128,512]{2,1,0:T(8,128)S(1)}, f32[2,128,512]{2,1,0:T(8,128)S(1)}, u32[]{:S(2)}, u32[]{:S(2)}) collective-permute-start(f32[2,128,512]{2,1,0:T(8,128)S(1)} %far_strip.3), channel_id=1, source_target_pairs={{32,0},{64,32},{96,64},{16,48},{48,80},{80,112},{33,1},{65,33},{97... | collective-permute-start | bytes 1572872 | tf_op jit(solution)/shard_map/ppermute | solution.py:564
  52.6 10.6 %collective-permute-start.9 = (f32[2,128,512]{2,1,0:T(8,128)S(1)}, f32[2,128,512]{2,1,0:T(8,128)S(1)}, u32[]{:S(2)}, u32[]{:S(2)}) collective-permute-start(f32[2,128,512]{2,1,0:T(8,128)S(1)} %mate_strip.3), channel_id=1, source_target_pairs={{0,16},{16,0},{32,48},{48,32},{64,80},{80,64},{96,112},{112,96},{1... | collective-permute-start | bytes 1572872 | tf_op jit(solution)/shard_map/ppermute | solution.py:568
  61.2 12.5 %collective-permute-start.8 = (f32[2,128,512]{2,1,0:T(8,128)S(1)}, f32[2,128,512]{2,1,0:T(8,128)S(1)}, u32[]{:S(2)}, u32[]{:S(2)}) collective-permute-start(f32[2,128,512]{2,1,0:T(8,128)S(1)} %mate_strip.2), channel_id=1, source_target_pairs={{0,16},{16,0},{32,48},{48,32},{64,80},{80,64},{96,112},{112,96},{1... | collective-permute-start | bytes 1572872 | tf_op jit(solution)/shard_map/ppermute | solution.py:571
  63.2 10.5 %copy-start.3 = (bf16[1,1,1,512,512]{4,3,2,1,0:T(8,128)(2,1)S(1)}, bf16[1,1,1,512,512]{4,3,2,1,0:T(8,128)(2,1)}, u32[]{:S(2)}) copy-start(bf16[1,1,1,512,512]{4,3,2,1,0:T(8,128)(2,1)} %param.10) | copy-start | bytes 1572868
  79.0 14.2 %collective-permute-start.12 = (f32[2,128,512]{2,1,0:T(8,128)S(1)}, f32[2,128,512]{2,1,0:T(8,128)S(1)}, u32[]{:S(2)}, u32[]{:S(2)}) collective-permute-start(f32[2,128,512]{2,1,0:T(8,128)S(1)} %get-tuple-element.97), channel_id=1, source_target_pairs={{0,16},{16,0},{32,48},{48,32},{64,80},{80,64},{96,112},{112,96},{1... | collective-permute-start | bytes 1572872 | tf_op jit(solution)/shard_map/ppermute | solution.py:592
  87.2 28.3 %collective-permute-start.10 = (f32[2,128,512]{2,1,0:T(8,128)S(1)}, f32[2,128,512]{2,1,0:T(8,128)S(1)}, u32[]{:S(2)}, u32[]{:S(2)}) collective-permute-start(f32[2,128,512]{2,1,0:T(8,128)S(1)} %get-tuple-element.96), channel_id=1, source_target_pairs={{0,16},{16,0},{32,48},{48,32},{64,80},{80,64},{96,112},{112,96},{1... | collective-permute-start | bytes 1572872 | tf_op jit(solution)/shard_map/ppermute | solution.py:593
  93.2 46.2 %collective-permute-start.13 = (f32[2,2,512,128]{3,2,1,0:T(8,128)S(1)}, f32[2,2,512,128]{3,2,1,0:T(8,128)S(1)}, u32[]{:S(2)}, u32[]{:S(2)}) collective-permute-start(f32[2,2,512,128]{3,2,1,0:T(8,128)S(1)} %get-tuple-element.101), channel_id=1, source_target_pairs={{0,1},{1,0},{2,3},{3,2},{4,5},{5,4},{6,7},{7,6},{8,9},{9,8},{10,11... | collective-permute-start | bytes 3145736 | tf_op jit(solution)/shard_map/ppermute | solution.py:543
  93.4 24.0 %collective-permute-start.17 = (f32[2,128,512]{2,1,0:T(8,128)S(1)}, f32[2,128,512]{2,1,0:T(8,128)S(1)}, u32[]{:S(2)}, u32[]{:S(2)}) collective-permute-start(f32[2,128,512]{2,1,0:T(8,128)S(1)} %collective-permute-done.12.mate.refs_4_), channel_id=1, source_target_pairs={{0,32},{32,64},{64,96},{48,16},{80,48},{112,80},{1,33},{33,65},{65... | collective-permute-start | bytes 1572872 | tf_op jit(solution)/shard_map/ppermute | solution.py:594
  96.0 43.4 %collective-permute-start.14 = (f32[2,2,512,128]{3,2,1,0:T(8,128)S(1)}, f32[2,2,512,128]{3,2,1,0:T(8,128)S(1)}, u32[]{:S(2)}, u32[]{:S(2)}) collective-permute-start(f32[2,2,512,128]{3,2,1,0:T(8,128)S(1)} %get-tuple-element.102), channel_id=1, source_target_pairs={{1,2},{3,4},{5,6},{7,8},{9,10},{11,12},{13,14},{2,1},{4,3},{6,5},{... | collective-permute-start | bytes 3145736 | tf_op jit(solution)/shard_map/ppermute | solution.py:542
  115.5 15.0 %collective-permute-start.11 = (f32[2,128,512]{2,1,0:T(8,128)S(1)}, f32[2,128,512]{2,1,0:T(8,128)S(1)}, u32[]{:S(2)}, u32[]{:S(2)}) collective-permute-start(f32[2,128,512]{2,1,0:T(8,128)S(1)} %collective-permute-done.10.mate.refs_4_), channel_id=1, source_target_pairs={{0,32},{32,64},{64,96},{48,16},{80,48},{112,80},{1,33},{33,65},{65... | collective-permute-start | bytes 1572872 | tf_op jit(solution)/shard_map/ppermute | solution.py:597
  118.2 16.3 %copy-start.4 = (f32[2]{0:T(128)S(1)}, f32[2]{0:T(128)}, u32[]{:S(2)}) copy-start(f32[2]{0:T(128)} %refs_1_.22) | copy-start | bytes 28
  118.2 14.4 %collective-permute-start.18 = (f32[2,256,128]{2,1,0:T(8,128)S(1)}, f32[2,256,128]{2,1,0:T(8,128)S(1)}, u32[]{:S(2)}, u32[]{:S(2)}) collective-permute-start(f32[2,256,128]{2,1,0:T(8,128)S(1)} %get-tuple-element.105), channel_id=1, source_target_pairs={{0,1},{1,0},{2,3},{3,2},{4,5},{5,4},{6,7},{7,6},{8,9},{9,8},{10,11... | collective-permute-start | bytes 786440 | tf_op jit(solution)/shard_map/ppermute | solution.py:543
  118.6 20.8 %collective-permute-start.19 = (f32[2,256,128]{2,1,0:T(8,128)S(1)}, f32[2,256,128]{2,1,0:T(8,128)S(1)}, u32[]{:S(2)}, u32[]{:S(2)}) collective-permute-start(f32[2,256,128]{2,1,0:T(8,128)S(1)} %get-tuple-element.106), channel_id=1, source_target_pairs={{1,2},{3,4},{5,6},{7,8},{9,10},{11,12},{13,14},{2,1},{4,3},{6,5},{... | collective-permute-start | bytes 786440 | tf_op jit(solution)/shard_map/ppermute | solution.py:542
  131.2 10.3 %collective-permute-start.15 = (f32[2,256,128]{2,1,0:T(8,128)S(1)}, f32[2,256,128]{2,1,0:T(8,128)S(1)}, u32[]{:S(2)}, u32[]{:S(2)}) collective-permute-start(f32[2,256,128]{2,1,0:T(8,128)S(1)} %get-tuple-element.103), channel_id=1, source_target_pairs={{0,1},{1,0},{2,3},{3,2},{4,5},{5,4},{6,7},{7,6},{8,9},{9,8},{10,11... | collective-permute-start | bytes 786440 | tf_op jit(solution)/shard_map/ppermute | solution.py:543
  132.5 9.2 %collective-permute-start.16 = (f32[2,256,128]{2,1,0:T(8,128)S(1)}, f32[2,256,128]{2,1,0:T(8,128)S(1)}, u32[]{:S(2)}, u32[]{:S(2)}) collective-permute-start(f32[2,256,128]{2,1,0:T(8,128)S(1)} %get-tuple-element.104), channel_id=1, source_target_pairs={{1,2},{3,4},{5,6},{7,8},{9,10},{11,12},{13,14},{2,1},{4,3},{6,5},{... | collective-permute-start | bytes 786440 | tf_op jit(solution)/shard_map/ppermute | solution.py:542
